TPU v7x, 32 devices: a whole 2x2x4 slice. The times are simulated.
32 devices in a mesh: groups: 2 (over y), cell: 4 (over z), member: 4 (over x, core).
Axes of the slice: x: 2, y: 2, z: 4, core: 2. Of those that a mesh axis runs over, the one named last changes fastest.
Arguments:
- prior_sample_set: float32 [512, 3, 32, 512], P(('groups', 'member'), None, 'cell'), parts along dimension 0, may hold values from -6 to 6
- wind_table: float32 [8, 2], replicated, may hold values from -0.45 to 0.45
- regimes: int32 [16, 4], P('groups'), parts along dimension 0, may hold values from 0 to 7
- obs_index: int32 [8, 512], P(('groups', 'cell')), parts along dimension 0, may hold values from 0 to 4095
- obs_count: int32 [8], P(('groups', 'cell')), parts along dimension 0, may hold values from 1 to 512, as said below
- obs_value: float32 [8, 512], P(('groups', 'cell')), parts along dimension 0, may hold values from -6 to 6
- obs_var: float32 [8, 512], P(('groups', 'cell')), parts along dimension 0, may hold values from 0.25 to 4
Outputs:
- posterior_sample_set: float32 [512, 3, 32, 512], P(('groups', 'member'), None, 'cell'), parts along dimension 0
There are 2 independent parts, one for each index of `groups`. A program takes and returns all parts, laid end to end along the dimension named above; an argument that names none is the same for every part. Nothing has to cross between parts.
Inputs may be any that keep to these rules, and one draw needn't show every extreme that they name: `obs_count`: some tile has exactly 512 live slots.
All inputs are finite; a program needn't handle non-finite values.
Results may differ from a plain program's by a relative error of at most 0.019.
The roundings to bfloat16 on the way count: a program that leaves them out, or rounds other values in their place, can miss the bound.
Values may be sent and summed in bfloat16 or wider, within the bound.
A program may use at most 64 MiB of HBM per device.

v0:
```python
import jax
import jax.numpy as jnp
from jax import lax
from jax.sharding import PartitionSpec as P

SUBSTEPS = 4
BAND = 4
ROOT_STEPS = 24


diffusion = 0.02


def padded_2(cells, sides, width):
    for axis, dim in sides:
        count = lax.axis_size(axis)
        ends = count - 1
        head = lax.slice_in_dim(cells, 0, width, axis=dim)
        tail = lax.slice_in_dim(cells, cells.shape[dim] - width, cells.shape[dim], axis=dim)
        cells = jnp.concatenate(
            [
                lax.ppermute(tail, axis, [(i, (i + 1) % count) for i in range(ends)]),
                cells,
                lax.ppermute(head, axis, [((i + 1) % count, i) for i in range(ends)]),
            ],
            axis=dim,
        )
    return cells


def row_speeds(row_ids, regime_column, wind_table, row_total):
    band_ids = jnp.clip(row_ids, 0, row_total - 1) // BAND
    band_hits = (band_ids[:, None] == jnp.arange(regime_column.shape[0])[None, :]).astype(jnp.int32)
    regime_ids = jnp.sum(band_hits * regime_column[None, :], axis=1)
    regime_hits = (regime_ids[:, None] == jnp.arange(wind_table.shape[0])[None, :]).astype(
        jnp.float32
    )
    speed = jnp.dot(
        regime_hits, wind_table, precision=lax.Precision.HIGHEST, preferred_element_type=jnp.float32
    )
    return (speed[:, 0:1], speed[:, 1:2])


def stencil(padded, speed_x, speed_y):
    centre = padded[..., 1:-1, :]
    south = padded[..., :-2, :]
    north = padded[..., 2:, :]
    widths = [(0, 0)] * (centre.ndim - 1) + [(1, 1)]
    sides = jnp.pad(centre, widths)
    west = sides[..., :-2]
    east = sides[..., 2:]
    result = (
        centre
        - jnp.maximum(speed_x, 0.0) * (centre - south)
        - jnp.minimum(speed_x, 0.0) * (north - centre)
    )
    result = (
        result
        - jnp.maximum(speed_y, 0.0) * (centre - west)
        - jnp.minimum(speed_y, 0.0) * (east - centre)
    )
    return result + diffusion * (north + south + east + west - 4.0 * centre)


def inverse_root(precision_matrix):
    size_n = precision_matrix.shape[0]
    identity = jnp.eye(size_n, dtype=jnp.float32)
    scale = jnp.trace(precision_matrix)
    start = (precision_matrix / scale, identity)

    def newton_step(index, carry):
        upper, lower = carry
        middle = 1.5 * identity - 0.5 * jnp.dot(
            lower, upper, precision=lax.Precision.HIGHEST, preferred_element_type=jnp.float32
        )
        upper = jnp.dot(
            upper, middle, precision=lax.Precision.HIGHEST, preferred_element_type=jnp.float32
        )
        lower = jnp.dot(
            middle, lower, precision=lax.Precision.HIGHEST, preferred_element_type=jnp.float32
        )
        return (upper, lower)

    upper, lower = lax.fori_loop(0, ROOT_STEPS, newton_step, start)
    return (lower, scale)


def analysis(gram, gain, members):
    identity = jnp.eye(members, dtype=jnp.float32)
    precision_matrix = gram + (members - 1.0) * identity
    root_inverse, scale = inverse_root(precision_matrix)
    half_way = jnp.dot(
        root_inverse, gain, precision=lax.Precision.HIGHEST, preferred_element_type=jnp.float32
    )
    mean_weights = (
        jnp.dot(
            root_inverse,
            half_way,
            precision=lax.Precision.HIGHEST,
            preferred_element_type=jnp.float32,
        )
        / scale
    )
    root = jnp.sqrt((members - 1.0) / scale) * root_inverse
    blend = mean_weights[:, None] + root
    transform = blend - jnp.mean(blend, axis=0, keepdims=True) + 1.0 / members
    return transform.astype(jnp.bfloat16)


def observation_terms(predicted, slot_ids, obs_count, obs_value, obs_var):
    ybar = jnp.mean(predicted, axis=0)
    spread = predicted - ybar[None, :]
    live = (slot_ids < obs_count).astype(jnp.float32)
    weight = live / jnp.sqrt(obs_var)
    scaled = spread * weight[None, :]
    gram_part = jnp.dot(
        scaled, scaled.T, precision=lax.Precision.HIGHEST, preferred_element_type=jnp.float32
    )
    innovation = weight * (obs_value - ybar)
    gain_part = jnp.dot(
        scaled, innovation, precision=lax.Precision.HIGHEST, preferred_element_type=jnp.float32
    )
    return (gram_part, gain_part)


def shards(prior_sample_set, wind_table, regimes, obs_index, obs_count, obs_value, obs_var):
    members_on_device = prior_sample_set.shape[0]
    tile_rows = prior_sample_set.shape[2]
    row_total = tile_rows * lax.axis_size("cell")
    first_row = lax.axis_index("cell") * tile_rows
    sample_set_values = prior_sample_set
    for step in range(SUBSTEPS):
        padded = padded_2(sample_set_values, (("cell", 2),), 1)
        row_ids = first_row + jnp.arange(tile_rows)
        speed_x, speed_y = row_speeds(row_ids, regimes[:, step], wind_table, row_total)
        sample_set_values = stencil(padded, speed_x, speed_y)
    first_cloud_cover = sample_set_values[:, 0].reshape(members_on_device, -1)
    slots_total = obs_index.shape[1]
    cell_hits = (jnp.arange(first_cloud_cover.shape[1])[:, None] == obs_index[0][None, :]).astype(
        jnp.float32
    )
    local_pred = jnp.dot(
        first_cloud_cover,
        cell_hits,
        precision=lax.Precision.HIGHEST,
        preferred_element_type=jnp.float32,
    )
    predicted = lax.all_gather(local_pred, "member", axis=0, tiled=True)
    slot_ids = jnp.arange(slots_total)
    gram_part, gain_part = observation_terms(
        predicted, slot_ids, obs_count[0], obs_value[0], obs_var[0]
    )
    gram, gain = lax.psum((gram_part, gain_part), "cell")
    members = gram.shape[0]
    update_matrix_reduced_precise = analysis(gram, gain, members)
    predicted_reduced_precise = sample_set_values.astype(jnp.bfloat16).reshape(
        members_on_device, prior_sample_set.shape[1], -1
    )
    my_columns = lax.dynamic_slice_in_dim(
        update_matrix_reduced_precise,
        lax.axis_index("member") * members_on_device,
        members_on_device,
        1,
    )
    initial = jnp.zeros(predicted_reduced_precise.shape, jnp.float32)
    piece = lax.all_gather(predicted_reduced_precise, "member", axis=0, tiled=True)
    coeffs = lax.slice_in_dim(my_columns, 0, piece.shape[0], axis=0)
    blended = initial + jnp.einsum("ij,ifc->jfc", coeffs, piece, preferred_element_type=jnp.float32)
    return blended.reshape(prior_sample_set.shape)


def solution(mesh):
    return jax.shard_map(
        shards,
        mesh=mesh,
        in_specs=(
            P(("groups", "member"), None, "cell", None),
            P(),
            P("groups", None),
            P(("groups", "cell"), None),
            P(("groups", "cell")),
            P(("groups", "cell"), None),
            P(("groups", "cell"), None),
        ),
        out_specs=P(("groups", "member"), None, "cell", None),
        check_vma=False,
    )
```

profile of v0, /device:TPU:0, one launch (start us, length us, event | category | flops | bytes accessed | tf_op | source)
XLA Modules:
  0.0 187.4 jit_solution(12085723953323743771)
XLA Ops:
  7.4 3.7 %copy.46 = f32[64,3,8,512]{3,0,2,1:T(8,128)S(1)} copy(f32[64,3,8,512]{3,2,1,0:T(8,128)} %param.9) | data formatting | bytes 6291456 | tf_op args[0]
  11.1 0.8 fusion.91
  11.9 5.7 %collective-permute-start = (f32[64,3,1,512]{3,0,2,1:T(8,128)}, f32[64,3,1,512]{3,0,2,1:T(8,128)}, u32[]{:S(2)}, u32[]{:S(2)}) collective-permute-start(f32[64,3,1,512]{3,0,2,1:T(8,128)} %get-tuple-element.68), channel_id=1, source_target_pairs={{0,4},{4,8},{8,12},{1,5},{5,9},{9,13},{2,6},{6,10},{10,14},{3,7},{... | collective-permute-start | bytes 1179656 | tf_op jit(solution)/shard_map/ppermute | solution.py:22
  17.6 1.3 collective-permute-start.1
  18.9 0.6 slice_bitcast_fusion.3
  20.2 0.9 select_reduce_fusion.1
  21.4 4.1 %collective-permute-done = f32[64,3,1,512]{3,0,2,1:T(8,128)} collective-permute-done((f32[64,3,1,512]{3,0,2,1:T(8,128)}, f32[64,3,1,512]{3,0,2,1:T(8,128)}, u32[]{:S(2)}, u32[]{:S(2)}) %collective-permute-start) | collective-permute-done | bytes 393248 | tf_op jit(solution)/shard_map/ppermute | solution.py:22
  25.5 4.6 %collective-permute-done.1 = f32[64,3,1,512]{3,0,2,1:T(8,128)} collective-permute-done((f32[64,3,1,512]{3,0,2,1:T(8,128)S(1)}, f32[64,3,1,512]{3,0,2,1:T(8,128)}, u32[]{:S(2)}, u32[]{:S(2)}) %collective-permute-start.1) | collective-permute-done | bytes 393248 | tf_op jit(solution)/shard_map/ppermute | solution.py:24
  30.2 4.2 %fusion.53 = f32[64,3,8,512]{3,0,2,1:T(8,128)S(1)} fusion(f32[64,3,1,512]{3,0,2,1:T(8,128)} %collective-permute-done.1, f32[64,3,8,512]{3,0,2,1:T(8,128)S(1)} %copy.46, f32[64,3,1,512]{3,0,2,1:T(8,128)} %collective-permute-done, f32[8]{0:T(128)S(1)} %get-tuple-element.92, f32[8]{0:T(128)S(1)} %get-tuple-element.93, f32[8]{0:T(128)S(1)} %get-tuple-element.91, ...), kind=kLoop, calls=%fused_computation.71 | loop fusion | flops 16515072 | bytes 7078016 | tf_op jit(solution)/shard_map/add | solution.py:62
  34.5 2.8 %collective-permute-start.2 = (f32[64,3,1,512]{3,0,2,1:T(8,128)S(1)}, f32[64,3,1,512]{3,0,2,1:T(8,128)S(1)}, u32[]{:S(2)}, u32[]{:S(2)}) collective-permute-start(f32[64,3,1,512]{3,0,2,1:T(8,128)S(1)} %get-tuple-element.66), channel_id=1, source_target_pairs={{0,4},{4,8},{8,12},{1,5},{5,9},{9,13},{2,6},{6,10},{10,14},{3,7},{... | collective-permute-start | bytes 1179656 | tf_op jit(solution)/shard_map/ppermute | solution.py:22
  37.2 1.3 collective-permute-start.3
  38.7 5.7 %collective-permute-done.2 = f32[64,3,1,512]{3,0,2,1:T(8,128)S(1)} collective-permute-done((f32[64,3,1,512]{3,0,2,1:T(8,128)S(1)}, f32[64,3,1,512]{3,0,2,1:T(8,128)S(1)}, u32[]{:S(2)}, u32[]{:S(2)}) %collective-permute-start.2) | collective-permute-done | bytes 393248 | tf_op jit(solution)/shard_map/ppermute | solution.py:22
  44.4 4.1 %collective-permute-done.3 = f32[64,3,1,512]{3,0,2,1:T(8,128)S(1)} collective-permute-done((f32[64,3,1,512]{3,0,2,1:T(8,128)S(1)}, f32[64,3,1,512]{3,0,2,1:T(8,128)S(1)}, u32[]{:S(2)}, u32[]{:S(2)}) %collective-permute-start.3) | collective-permute-done | bytes 393248 | tf_op jit(solution)/shard_map/ppermute | solution.py:24
  48.5 3.1 %fusion.39 = f32[64,3,8,512]{3,0,2,1:T(8,128)S(1)} fusion(f32[64,3,1,512]{3,0,2,1:T(8,128)S(1)} %collective-permute-done.3, f32[64,3,8,512]{3,0,2,1:T(8,128)S(1)} %fusion.53, f32[64,3,1,512]{3,0,2,1:T(8,128)S(1)} %collective-permute-done.2, f32[8]{0:T(128)S(1)} %get-tuple-element.88, f32[8]{0:T(128)S(1)} %get-tuple-element.89, f32[8]{0:T(128)S(1)} %get-tuple-element.87, ...), kind=kLoop, calls=%fused_computation.55 | loop fusion | flops 16515072 | bytes 7078016 | tf_op jit(solution)/shard_map/add | solution.py:62
  51.7 3.5 %collective-permute-start.4 = (f32[64,3,1,512]{3,0,2,1:T(8,128)S(1)}, f32[64,3,1,512]{3,0,2,1:T(8,128)S(1)}, u32[]{:S(2)}, u32[]{:S(2)}) collective-permute-start(f32[64,3,1,512]{3,0,2,1:T(8,128)S(1)} %get-tuple-element.64), channel_id=1, source_target_pairs={{0,4},{4,8},{8,12},{1,5},{5,9},{9,13},{2,6},{6,10},{10,14},{3,7},{... | collective-permute-start | bytes 1179656 | tf_op jit(solution)/shard_map/ppermute | solution.py:22
  55.2 1.3 collective-permute-start.5
  56.7 4.4 %collective-permute-done.4 = f32[64,3,1,512]{3,0,2,1:T(8,128)S(1)} collective-permute-done((f32[64,3,1,512]{3,0,2,1:T(8,128)S(1)}, f32[64,3,1,512]{3,0,2,1:T(8,128)S(1)}, u32[]{:S(2)}, u32[]{:S(2)}) %collective-permute-start.4) | collective-permute-done | bytes 393248 | tf_op jit(solution)/shard_map/ppermute | solution.py:22
  61.1 4.1 %collective-permute-done.5 = f32[64,3,1,512]{3,0,2,1:T(8,128)S(1)} collective-permute-done((f32[64,3,1,512]{3,0,2,1:T(8,128)S(1)}, f32[64,3,1,512]{3,0,2,1:T(8,128)S(1)}, u32[]{:S(2)}, u32[]{:S(2)}) %collective-permute-start.5) | collective-permute-done | bytes 393248 | tf_op jit(solution)/shard_map/ppermute | solution.py:24
  65.3 3.2 %fusion.25 = f32[64,3,8,512]{3,0,2,1:T(8,128)S(1)} fusion(f32[64,3,1,512]{3,0,2,1:T(8,128)S(1)} %collective-permute-done.5, f32[64,3,8,512]{3,0,2,1:T(8,128)S(1)} %fusion.39, f32[64,3,1,512]{3,0,2,1:T(8,128)S(1)} %collective-permute-done.4, f32[8]{0:T(128)S(1)} %get-tuple-element.84, f32[8]{0:T(128)S(1)} %get-tuple-element.85, f32[8]{0:T(128)S(1)} %get-tuple-element.83, ...), kind=kLoop, calls=%fused_computation.39 | loop fusion | flops 16515072 | bytes 7078016 | tf_op jit(solution)/shard_map/add | solution.py:62
  68.5 2.5 %collective-permute-start.6 = (f32[64,3,1,512]{3,0,2,1:T(8,128)S(1)}, f32[64,3,1,512]{3,0,2,1:T(8,128)S(1)}, u32[]{:S(2)}, u32[]{:S(2)}) collective-permute-start(f32[64,3,1,512]{3,0,2,1:T(8,128)S(1)} %get-tuple-element.62), channel_id=1, source_target_pairs={{0,4},{4,8},{8,12},{1,5},{5,9},{9,13},{2,6},{6,10},{10,14},{3,7},{... | collective-permute-start | bytes 1179656 | tf_op jit(solution)/shard_map/ppermute | solution.py:22
  71.0 1.3 collective-permute-start.7
  72.4 3.9 %collective-permute-done.6 = f32[64,3,1,512]{3,0,2,1:T(8,128)S(1)} collective-permute-done((f32[64,3,1,512]{3,0,2,1:T(8,128)S(1)}, f32[64,3,1,512]{3,0,2,1:T(8,128)S(1)}, u32[]{:S(2)}, u32[]{:S(2)}) %collective-permute-start.6) | collective-permute-done | bytes 393248 | tf_op jit(solution)/shard_map/ppermute | solution.py:22
  76.3 4.4 %collective-permute-done.7 = f32[64,3,1,512]{3,0,2,1:T(8,128)S(1)} collective-permute-done((f32[64,3,1,512]{3,0,2,1:T(8,128)S(1)}, f32[64,3,1,512]{3,0,2,1:T(8,128)S(1)}, u32[]{:S(2)}, u32[]{:S(2)}) %collective-permute-start.7) | collective-permute-done | bytes 393248 | tf_op jit(solution)/shard_map/ppermute | solution.py:24
  80.7 3.4 %convert_bitcast_fusion = (bf16[3,8,8,8,512]{4,3,2,1,0:T(8,128)(2,1)S(1)}, f32[64,3,8,512]{3,0,2,1:T(8,128)S(1)}) fusion(f32[64,3,8,512]{3,0,2,1:T(8,128)S(1)} %fusion.25, f32[8]{0:T(128)S(1)} %get-tuple-element.80, f32[8]{0:T(128)S(1)} %get-tuple-element.81, f32[64,3,1,512]{3,0,2,1:T(8,128)S(1)} %collective-permute-done.7, f32[8]{0:T(128)S(1)} %get-tuple-element.79, ...), kind=kLoop, calls=%fused_computation.80 | loop fusion | flops 17301504 | bytes 8650880
  84.2 0.5 copy-done.4
  84.7 3.0 %fusion.3 = f32[64,512]{1,0:T(8,128)S(1)} fusion(f32[64,4096]{1,0:T(8,128)S(1)} %bitcast.108, s32[512]{0:T(512)S(1)} %bitcast.117), kind=kOutput, calls=%fused_computation.6 | convolution fusion | flops 1612709888 | bytes 1181696 | tf_op jit(solution)/shard_map/dot_general | solution.py:142
  87.8 7.4 %all_gather.6 = f32[256,512]{1,0:T(8,128)S(1)} all-gather(f32[64,512]{1,0:T(8,128)S(1)} %fusion.3), channel_id=1, replica_groups=mesh['groups'=2,'cell'=4,'member'=4] {'member'}, dimensions={0}, use_global_device_ids=true | all-gather | bytes 655360 | tf_op jit(solution)/shard_map/all_gather | solution.py:148
  95.2 1.4 fusion.62
  96.7 1.3 copy.59
  98.0 0.5 fusion.61
  98.5 8.6 %psum.15 = f32[256]{0:T(256)S(1)} all-reduce(f32[256]{0:T(256)S(1)} %bitcast.114), channel_id=1, replica_groups=mesh['groups'=2,'cell'=4,'member'=4] {'cell'}, use_global_device_ids=true, to_apply=%region_9.10 | all-reduce | flops 256 | bytes 2048 | tf_op jit(solution)/shard_map/psum | solution.py:153
  107.2 22.7 %all-reduce.6.cloned.1.call-done = f32[256,256]{1,0:T(8,128)} async-done(((f32[256,256]{1,0:T(8,128)}), f32[256,256]{1,0:T(8,128)}) %all-reduce.6.cloned.1.call-update) | async-done | bytes 262160 | tf_op jit(solution)/shard_map/psum | solution.py:153
  129.9 1.7 select_reduce_fusion
  131.6 1.7 fusion.68
  133.4 35.4 %while.13 = (s32[]{:T(128)}, f32[256,256]{0,1:T(8,128)S(1)}, f32[256,256]{1,0:T(8,128)S(1)}, s32[]{:T(128)}) while((s32[]{:T(128)}, f32[256,256]{0,1:T(8,128)S(1)}, f32[256,256]{1,0:T(8,128)S(1)}, s32[]{:T(128)}) %tuple.51), condition=%wide.region_8.9_spmd.clone, body=%wide.region_7.8_spmd.clone.sunk | while | flops 604241920 | bytes 3407925 | solution.py:84
  133.4 0.4 fusion.126
  134.2 0.6 convolution_bitcast_fusion.3
  135.7 0.6 convolution_bitcast_fusion.3
  137.2 0.6 convolution_bitcast_fusion.3
  138.7 0.6 convolution_bitcast_fusion.3
  140.1 0.6 convolution_bitcast_fusion.3
  141.6 0.6 convolution_bitcast_fusion.3
  143.1 0.6 convolution_bitcast_fusion.3
  144.6 0.6 convolution_bitcast_fusion.3
  146.0 0.6 convolution_bitcast_fusion.3
  147.5 0.6 convolution_bitcast_fusion.3
  149.0 0.6 convolution_bitcast_fusion.3
  150.4 0.6 convolution_bitcast_fusion.3
  151.9 0.6 convolution_bitcast_fusion.3
  153.4 0.6 convolution_bitcast_fusion.3
  154.9 0.6 convolution_bitcast_fusion.3
  156.3 0.6 convolution_bitcast_fusion.3
  157.8 0.6 convolution_bitcast_fusion.3
  159.3 0.6 convolution_bitcast_fusion.3
  160.8 0.6 convolution_bitcast_fusion.3
  162.2 0.6 convolution_bitcast_fusion.3
  163.7 0.6 convolution_bitcast_fusion.3
  165.2 0.6 convolution_bitcast_fusion.3
  166.7 0.6 convolution_bitcast_fusion.3
  168.1 0.6 convolution_bitcast_fusion.3
  170.3 0.7 broadcast_divide_fusion
  171.2 4.0 %fusion.72 = f32[64,3,4096]{2,0,1:T(8,128)S(1)} fusion(bf16[256,3,4096]{2,0,1:T(8,128)(2,1)} %all-gather.2.cloned.1.call-done, f32[256,256]{0,1:T(8,128)S(1)} %get-tuple-element.59, s32[]{:T(128)S(6)} %select_n.22, f32[64]{0:T(128)S(1)} %dynamic-slice), kind=kOutput, calls=%fused_computation.99 | convolution fusion | flops 402702336 | bytes 9503236 | tf_op jit(solution)/shard_map/ij,ifc->jfc/dot_general | solution.py:168
  175.3 2.7 %copy.61 = f32[24,8,8,512]{3,2,1,0:T(8,128)S(1)} copy(f32[24,8,8,512]{3,1,2,0:T(8,128)S(1)} %bitcast.105) | data formatting | bytes 6291456
  178.0 2.0 %copy.58 = f32[64,3,8,512]{3,2,1,0:T(8,128)} copy(f32[64,3,8,512]{3,2,0,1:T(8,128)S(1)} %bitcast.106) | data formatting | bytes 6291456 | tf_op jit(solution)/shard_map/reshape | solution.py:169
  (134 shorter events, 21.7 us)
Async XLA Ops:
  7.4 13.7 %copy-start = (f32[8,2]{0,1:T(2,128)S(1)}, f32[8,2]{0,1:T(2,128)}, u32[]{:S(2)}) copy-start(f32[8,2]{0,1:T(2,128)} %param.10) | copy-start | bytes 196
  7.4 11.5 %copy-start.1 = (s32[8,4]{0,1:T(4,128)S(1)}, s32[8,4]{0,1:T(4,128)}, u32[]{:S(2)}) copy-start(s32[8,4]{0,1:T(4,128)} %param.11) | copy-start | bytes 388
  7.4 122.5 %all-reduce.6.cloned.1.call-start = ((), (), s32[]{:S(2)}) async-start(), calls=%async_computation | async-start | bytes 524288 | tf_op jit(solution)/shard_map/psum | solution.py:153
  11.9 13.6 %collective-permute-start = (f32[64,3,1,512]{3,0,2,1:T(8,128)}, f32[64,3,1,512]{3,0,2,1:T(8,128)}, u32[]{:S(2)}, u32[]{:S(2)}) collective-permute-start(f32[64,3,1,512]{3,0,2,1:T(8,128)} %get-tuple-element.68), channel_id=1, source_target_pairs={{0,4},{4,8},{8,12},{1,5},{5,9},{9,13},{2,6},{6,10},{10,14},{3,7},{... | collective-permute-start | bytes 1179656 | tf_op jit(solution)/shard_map/ppermute | solution.py:22
  17.6 12.6 %collective-permute-start.1 = (f32[64,3,1,512]{3,0,2,1:T(8,128)S(1)}, f32[64,3,1,512]{3,0,2,1:T(8,128)}, u32[]{:S(2)}, u32[]{:S(2)}) collective-permute-start(f32[64,3,1,512]{3,0,2,1:T(8,128)S(1)} %get-tuple-element.69), channel_id=1, source_target_pairs={{4,0},{8,4},{12,8},{5,1},{9,5},{13,9},{6,2},{10,6},{14,10},{7,3},{... | collective-permute-start | bytes 1179656 | tf_op jit(solution)/shard_map/ppermute | solution.py:24
  34.5 9.9 %collective-permute-start.2 = (f32[64,3,1,512]{3,0,2,1:T(8,128)S(1)}, f32[64,3,1,512]{3,0,2,1:T(8,128)S(1)}, u32[]{:S(2)}, u32[]{:S(2)}) collective-permute-start(f32[64,3,1,512]{3,0,2,1:T(8,128)S(1)} %get-tuple-element.66), channel_id=1, source_target_pairs={{0,4},{4,8},{8,12},{1,5},{5,9},{9,13},{2,6},{6,10},{10,14},{3,7},{... | collective-permute-start | bytes 1179656 | tf_op jit(solution)/shard_map/ppermute | solution.py:22
  37.2 11.3 %collective-permute-start.3 = (f32[64,3,1,512]{3,0,2,1:T(8,128)S(1)}, f32[64,3,1,512]{3,0,2,1:T(8,128)S(1)}, u32[]{:S(2)}, u32[]{:S(2)}) collective-permute-start(f32[64,3,1,512]{3,0,2,1:T(8,128)S(1)} %get-tuple-element.67), channel_id=1, source_target_pairs={{4,0},{8,4},{12,8},{5,1},{9,5},{13,9},{6,2},{10,6},{14,10},{7,3},{... | collective-permute-start | bytes 1179656 | tf_op jit(solution)/shard_map/ppermute | solution.py:24
  51.7 9.4 %collective-permute-start.4 = (f32[64,3,1,512]{3,0,2,1:T(8,128)S(1)}, f32[64,3,1,512]{3,0,2,1:T(8,128)S(1)}, u32[]{:S(2)}, u32[]{:S(2)}) collective-permute-start(f32[64,3,1,512]{3,0,2,1:T(8,128)S(1)} %get-tuple-element.64), channel_id=1, source_target_pairs={{0,4},{4,8},{8,12},{1,5},{5,9},{9,13},{2,6},{6,10},{10,14},{3,7},{... | collective-permute-start | bytes 1179656 | tf_op jit(solution)/shard_map/ppermute | solution.py:22
  55.2 10.1 %collective-permute-start.5 = (f32[64,3,1,512]{3,0,2,1:T(8,128)S(1)}, f32[64,3,1,512]{3,0,2,1:T(8,128)S(1)}, u32[]{:S(2)}, u32[]{:S(2)}) collective-permute-start(f32[64,3,1,512]{3,0,2,1:T(8,128)S(1)} %get-tuple-element.65), channel_id=1, source_target_pairs={{4,0},{8,4},{12,8},{5,1},{9,5},{13,9},{6,2},{10,6},{14,10},{7,3},{... | collective-permute-start | bytes 1179656 | tf_op jit(solution)/shard_map/ppermute | solution.py:24
  65.3 7.1 %copy-start.2 = (f32[1,512]{1,0:T(1,128)S(1)}, f32[1,512]{1,0:T(1,128)}, u32[]{:S(2)}) copy-start(f32[1,512]{1,0:T(1,128)} %param.15) | copy-start | bytes 6148
  68.5 7.7 %collective-permute-start.6 = (f32[64,3,1,512]{3,0,2,1:T(8,128)S(1)}, f32[64,3,1,512]{3,0,2,1:T(8,128)S(1)}, u32[]{:S(2)}, u32[]{:S(2)}) collective-permute-start(f32[64,3,1,512]{3,0,2,1:T(8,128)S(1)} %get-tuple-element.62), channel_id=1, source_target_pairs={{0,4},{4,8},{8,12},{1,5},{5,9},{9,13},{2,6},{6,10},{10,14},{3,7},{... | collective-permute-start | bytes 1179656 | tf_op jit(solution)/shard_map/ppermute | solution.py:22
  71.0 9.7 %collective-permute-start.7 = (f32[64,3,1,512]{3,0,2,1:T(8,128)S(1)}, f32[64,3,1,512]{3,0,2,1:T(8,128)S(1)}, u32[]{:S(2)}, u32[]{:S(2)}) collective-permute-start(f32[64,3,1,512]{3,0,2,1:T(8,128)S(1)} %get-tuple-element.63), channel_id=1, source_target_pairs={{4,0},{8,4},{12,8},{5,1},{9,5},{13,9},{6,2},{10,6},{14,10},{7,3},{... | collective-permute-start | bytes 1179656 | tf_op jit(solution)/shard_map/ppermute | solution.py:24
  84.1 0.7 copy-start.4
  84.1 11.1 %copy-start.3 = (f32[1,512]{1,0:T(1,128)S(1)}, f32[1,512]{1,0:T(1,128)}, u32[]{:S(2)}) copy-start(f32[1,512]{1,0:T(1,128)} %param.14) | copy-start | bytes 6148
  96.6 74.6 %all-gather.2.cloned.1.call-start = ((), (), s32[]{:S(2)}) async-start(), calls=%async_computation.1 | async-start | bytes 7864320 | tf_op jit(solution)/shard_map/all_gather | solution.py:166
Sparse Core Ops, SparseCore 0:
  96.7 33.1 all-reduce.5
Sparse Core Ops, SparseCore 1:
  107.3 44.9 all-gather.1
where the time goes:
time: 188 us; the launch traced here: 187 us
  waiting for transfers between devices  58.2 us (31%)
  matrix products  43.5 us (23%)
  starting transfers between devices  19.6 us (10%)
  other arithmetic  19.1 us (10%)
  between operations  16.5 us (9%)
  blocking collectives  16 us (9%)
  local copies, waits for them, and re-layouts  13.2 us (7%)
    psum x1, waiting for transfers between devices, shards(): gram, gain = lax.psum((gram_part, gain_part), 'cell')  22.7 us
    ppermute x4, waiting for transfers between devices, padded_2(): lax.ppermute(tail, axis, [(i, (i + 1) % count) for i in range(ends)])  18.1 us
    ppermute x4, waiting for transfers between devices, padded_2(): lax.ppermute(head, axis, [((i + 1) % count, i) for i in range(ends)])  17.3 us
    ppermute x4, starting transfers between devices, padded_2(): lax.ppermute(tail, axis, [(i, (i + 1) % count) for i in range(ends)])  14.4 us
    dot_general x24, matrix products, newton_step(): jnp.dot(upper, middle, precision=lax.Precision.HIGHEST, preferred_element...  14.3 us
    add x3, other arithmetic, stencil(): return result + diffusion * (north + south + east + west - 4.0 * centre)  10.5 us
    dot_general x24, matrix products, newton_step(): jnp.dot(lower, upper, precision=lax.Precision.HIGHEST, preferred_element_...  9.83 us
    dot_general x24, matrix products, newton_step(): jnp.dot(middle, lower, precision=lax.Precision.HIGHEST, preferred_element...  9.07 us
  transfers between devices with their start and end apart: 10, of which 9 were waited for; matrix products, arithmetic and copies ran while one was open for 23% of the time, Pallas kernels for 0%

commit v1 on v0

v1 whole, which is shorter than its diff:
```python
import functools

import jax
import jax.numpy as jnp
from jax import lax
from jax.experimental import pallas as pl
from jax.experimental.pallas import tpu as pltpu
from jax.sharding import PartitionSpec as P

SUBSTEPS = 4
BAND = 4
ROOT_STEPS = 24
HALO = SUBSTEPS
DIFFUSION = 0.02
MESH = pl.DeviceIdType.MESH
HIGHEST = lax.Precision.HIGHEST
VMEM_LIMIT = 48 * 1024 * 1024


def stencil_coeffs(regimes, wind_table, first_row, tile_rows, row_total):
    row_ids = first_row - HALO + jnp.arange(tile_rows + 2 * HALO)
    band_ids = jnp.clip(row_ids, 0, row_total - 1) // BAND
    band_hits = band_ids[:, None, None] == jnp.arange(regimes.shape[0])[None, :, None]
    ids = jnp.sum(jnp.where(band_hits, regimes[None], 0), axis=1)
    hits = ids[:, :, None, None] == jnp.arange(wind_table.shape[0])[None, None, :, None]
    speed = jnp.sum(jnp.where(hits, wind_table[None, None], 0.0), axis=2)
    cx, cy = speed[:, :, 0], speed[:, :, 1]
    parts = [
        1.0 - jnp.abs(cx) - jnp.abs(cy) - 4.0 * DIFFUSION,
        jnp.maximum(cx, 0.0) + DIFFUSION,
        DIFFUSION - jnp.minimum(cx, 0.0),
        jnp.maximum(cy, 0.0) + DIFFUSION,
        DIFFUSION - jnp.minimum(cy, 0.0),
    ]
    inside = (row_ids >= 0) & (row_ids < row_total)
    table = jnp.where(inside[:, None, None], jnp.stack(parts, axis=2), 0.0)
    return table.reshape(row_ids.shape[0], SUBSTEPS * 5).T


def stencil_kernel(chunk, with_obs, coeff_ref, *refs):
    if with_obs:
        index_ref, x_ref, south_ref, north_ref, out_ref, pred_ref, keep = refs
    else:
        x_ref, south_ref, north_ref, out_ref = refs
    rows, members, width = x_ref.shape[1:]
    lane = lax.broadcasted_iota(jnp.int32, (chunk, width), 1)

    def one_chunk(step_at, carry):
        at = pl.ds(pl.multiple_of(step_at * chunk, chunk), chunk)
        cells = [south_ref[0, i, at, :].astype(jnp.float32) for i in range(HALO)]
        cells += [x_ref[0, i, at, :] for i in range(rows)]
        cells += [north_ref[0, i, at, :].astype(jnp.float32) for i in range(HALO)]
        for s in range(SUBSTEPS):
            fresh = list(cells)
            for i in range(s + 1, rows + 2 * HALO - s - 1):
                q = cells[i]
                west = jnp.where(lane == 0, 0.0, pltpu.roll(q, 1, 1))
                east = jnp.where(lane == width - 1, 0.0, pltpu.roll(q, width - 1, 1))
                fresh[i] = (
                    q * coeff_ref[s * 5, i]
                    + cells[i - 1] * coeff_ref[s * 5 + 1, i]
                    + cells[i + 1] * coeff_ref[s * 5 + 2, i]
                    + west * coeff_ref[s * 5 + 3, i]
                    + east * coeff_ref[s * 5 + 4, i]
                )
            cells = fresh
        for i in range(rows):
            out_ref[0, i, at, :] = cells[HALO + i].astype(jnp.bfloat16)
            if with_obs:
                keep[i, at, :] = cells[HALO + i]
        return carry

    lax.fori_loop(0, members // chunk, one_chunk, 0)
    if with_obs:
        slots = index_ref.shape[1]
        column = lax.broadcasted_iota(jnp.int32, (width, slots), 0)
        pred_ref[...] = jnp.zeros_like(pred_ref)

        def one_row(i, carry):
            hits = jnp.where(column == index_ref[...] - i * width, 1.0, 0.0).astype(jnp.bfloat16)
            value = keep[i]
            high = value.astype(jnp.bfloat16)
            rest = value - high.astype(jnp.float32)
            middle = rest.astype(jnp.bfloat16)
            low = (rest - middle.astype(jnp.float32)).astype(jnp.bfloat16)
            picked = jnp.dot(
                jnp.concatenate([high, middle, low], axis=0),
                hits,
                preferred_element_type=jnp.float32,
            )
            pred_ref[...] += (
                picked[:members] + picked[members : 2 * members] + picked[2 * members :]
            )
            return carry

        lax.fori_loop(0, rows, one_row, 0)


def stencil_call(coeffs, cells, south, north, obs_index=None):
    fields, rows, members, width = cells.shape
    with_obs = obs_index is not None
    chunk = 16
    block = lambda r: pl.BlockSpec((1, r, members, width), lambda f: (f, 0, 0, 0))
    in_specs = [pl.BlockSpec(memory_space=pltpu.SMEM)]
    args = [coeffs]
    out_shape = [jax.ShapeDtypeStruct(cells.shape, jnp.bfloat16)]
    out_specs = [block(rows)]
    scratch = []
    if with_obs:
        slots = obs_index.shape[1]
        in_specs.append(pl.BlockSpec((1, slots), lambda f: (0, 0)))
        args.append(obs_index)
        out_shape.append(jax.ShapeDtypeStruct((members, slots), jnp.float32))
        out_specs.append(pl.BlockSpec((members, slots), lambda f: (0, 0)))
        scratch.append(pltpu.VMEM((rows, members, width), jnp.float32))
    return pl.pallas_call(
        functools.partial(stencil_kernel, chunk, with_obs),
        grid=(fields,),
        in_specs=in_specs + [block(rows), block(HALO), block(HALO)],
        out_specs=out_specs,
        out_shape=out_shape,
        scratch_shapes=scratch,
        compiler_params=pltpu.CompilerParams(vmem_limit_bytes=VMEM_LIMIT),
        cost_estimate=pl.CostEstimate(
            flops=fields * 60 * members * width * 12,
            bytes_accessed=fields * members * width * rows * 8,
            transcendentals=0,
        ),
    )(*args, cells, south, north)


def nt_dot(a, b):
    return lax.dot_general(
        a, b, (((1,), (1,)), ((), ())), precision=HIGHEST, preferred_element_type=jnp.float32
    )


def nn_dot(a, b):
    return jnp.dot(a, b, precision=HIGHEST, preferred_element_type=jnp.float32)


def analysis_kernel(
    n_cell,
    n_member,
    pred_ref,
    weight_ref,
    value_ref,
    out_ref,
    everyone,
    mine,
    others,
    total,
    gram,
    upper,
    lower,
    send_pred,
    recv_pred,
    send_part,
    recv_part,
    send_gram,
    recv_gram,
):
    cell = lax.axis_index("cell")
    member = lax.axis_index("member")
    count = pred_ref.shape[0]
    members = count * n_member

    barrier = pltpu.get_barrier_semaphore()
    for d in range(1, n_member):
        pl.semaphore_signal(
            barrier, inc=1, device_id={"member": lax.rem(member + d, n_member)}, device_id_type=MESH
        )
    for d in range(1, n_cell):
        pl.semaphore_signal(
            barrier, inc=1, device_id={"cell": lax.rem(cell + d, n_cell)}, device_id_type=MESH
        )
    pl.semaphore_wait(barrier, n_member + n_cell - 2)

    own = pl.ds(pl.multiple_of(member * count, count), count)
    copies = []
    for d in range(1, n_member):
        copy = pltpu.make_async_remote_copy(
            src_ref=pred_ref,
            dst_ref=everyone.at[own],
            send_sem=send_pred.at[d],
            recv_sem=recv_pred.at[d],
            device_id={"member": lax.rem(member + d, n_member)},
            device_id_type=MESH,
        )
        copy.start()
        copies.append(copy)
    everyone[own, :] = pred_ref[...]
    for copy in copies:
        copy.wait()

    predicted = everyone[...]
    ybar = jnp.mean(predicted, axis=0, keepdims=True)
    weight = weight_ref[...]
    scaled = (predicted - ybar) * weight
    local = (pred_ref[...] - ybar) * weight
    innovation = jnp.broadcast_to(weight * (value_ref[...] - ybar), (8, weight.shape[1]))
    mine[...] = nt_dot(jnp.concatenate([local, innovation], axis=0), scaled)

    copies = []
    for d in range(1, n_cell):
        copy = pltpu.make_async_remote_copy(
            src_ref=mine,
            dst_ref=others.at[d - 1],
            send_sem=send_part.at[d],
            recv_sem=recv_part.at[d],
            device_id={"cell": lax.rem(cell + d, n_cell)},
            device_id_type=MESH,
        )
        copy.start()
        copies.append(copy)
    for copy in copies:
        copy.wait()
    summed = mine[...]
    for d in range(n_cell - 1):
        summed = summed + others[d]
    total[...] = summed

    copies = []
    for d in range(1, n_member):
        copy = pltpu.make_async_remote_copy(
            src_ref=total.at[pl.ds(0, count)],
            dst_ref=gram.at[own],
            send_sem=send_gram.at[d],
            recv_sem=recv_gram.at[d],
            device_id={"member": lax.rem(member + d, n_member)},
            device_id_type=MESH,
        )
        copy.start()
        copies.append(copy)
    gram[own, :] = total[pl.ds(0, count), :]
    for copy in copies:
        copy.wait()

    rows = lax.broadcasted_iota(jnp.int32, (members, members), 0)
    columns = lax.broadcasted_iota(jnp.int32, (members, members), 1)
    identity = jnp.where(rows == columns, 1.0, 0.0).astype(jnp.float32)
    precision = gram[...] + (members - 1.0) * identity
    scale = jnp.sum(jnp.sum(precision * identity, axis=1, keepdims=True), axis=0, keepdims=True)
    upper[...] = precision / scale
    lower[...] = identity

    def newton(step, carry):
        middle = 1.5 * identity - 0.5 * nn_dot(lower[...], upper[...])
        upper[...] = nn_dot(upper[...], middle)
        lower[...] = nn_dot(middle, lower[...])
        return carry

    lax.fori_loop(0, ROOT_STEPS, newton, 0)

    gain = total[pl.ds(count, 8), :]
    half_way = nt_dot(gain, lower[...])
    mean_weights = nt_dot(half_way, lower[...])[0:1, :] / scale
    root = jnp.sqrt((members - 1.0) / scale) * lower[own, :]
    blend = mean_weights + root
    transform = blend - jnp.mean(blend, axis=1, keepdims=True) + 1.0 / members
    out_ref[...] = transform.astype(jnp.bfloat16)


def analysis_call(local_pred, weight, value):
    n_cell, n_member = lax.axis_size("cell"), lax.axis_size("member")
    count, slots = local_pred.shape
    members = count * n_member
    vmem = pl.BlockSpec(memory_space=pltpu.VMEM)
    dma = pltpu.SemaphoreType.DMA
    return pl.pallas_call(
        functools.partial(analysis_kernel, n_cell, n_member),
        out_shape=jax.ShapeDtypeStruct((count, members), jnp.bfloat16),
        in_specs=[vmem] * 3,
        out_specs=vmem,
        scratch_shapes=[
            pltpu.VMEM((members, slots), jnp.float32),
            pltpu.VMEM((count + 8, members), jnp.float32),
            pltpu.VMEM((n_cell - 1, count + 8, members), jnp.float32),
            pltpu.VMEM((count + 8, members), jnp.float32),
            pltpu.VMEM((members, members), jnp.float32),
            pltpu.VMEM((members, members), jnp.float32),
            pltpu.VMEM((members, members), jnp.float32),
            dma((n_member,)),
            dma((n_member,)),
            dma((n_cell,)),
            dma((n_cell,)),
            dma((n_member,)),
            dma((n_member,)),
        ],
        compiler_params=pltpu.CompilerParams(
            collective_id=0, has_side_effects=True, vmem_limit_bytes=16 * 1024 * 1024
        ),
        cost_estimate=pl.CostEstimate(
            flops=ROOT_STEPS * 3 * 12 * members**3, bytes_accessed=1 << 20, transcendentals=0
        ),
    )(local_pred, weight, value)


def blend_kernel(coeff_ref, piece_ref, out_ref):
    n_member, _, rows, count, width = piece_ref.shape
    for r in range(rows):
        block = piece_ref[:, 0, r].reshape(n_member * count, width)
        out_ref[0, r] = jnp.dot(coeff_ref[...], block, preferred_element_type=jnp.float32)


def blend_call(transform, piece):
    n_member, fields, rows, count, width = piece.shape
    group = rows // 2 if rows % 2 == 0 else rows
    return pl.pallas_call(
        blend_kernel,
        grid=(fields, rows // group),
        in_specs=[
            pl.BlockSpec(transform.shape, lambda f, r: (0, 0)),
            pl.BlockSpec((n_member, 1, group, count, width), lambda f, r: (0, f, r, 0, 0)),
        ],
        out_specs=pl.BlockSpec((1, group, count, width), lambda f, r: (f, r, 0, 0)),
        out_shape=jax.ShapeDtypeStruct((fields, rows, count, width), jnp.float32),
        compiler_params=pltpu.CompilerParams(vmem_limit_bytes=VMEM_LIMIT),
    )(transform, piece)


def halos(cells):
    n_cell = lax.axis_size("cell")
    rows = cells.shape[1]
    up = [(i, i + 1) for i in range(n_cell - 1)]
    down = [(i + 1, i) for i in range(n_cell - 1)]
    south = lax.ppermute(cells[:, rows - HALO :].astype(jnp.bfloat16), "cell", up)
    north = lax.ppermute(cells[:, :HALO].astype(jnp.bfloat16), "cell", down)
    return south, north


def shards(prior_sample_set, wind_table, regimes, obs_index, obs_count, obs_value, obs_var):
    tile_rows = prior_sample_set.shape[2]
    row_total = tile_rows * lax.axis_size("cell")
    first_row = lax.axis_index("cell") * tile_rows
    coeffs = stencil_coeffs(regimes, wind_table, first_row, tile_rows, row_total)
    live = jnp.arange(obs_var.shape[1])[None, :] < obs_count[0]
    weight = live.astype(jnp.float32) / jnp.sqrt(obs_var)

    cells = prior_sample_set.transpose(1, 2, 0, 3)
    south, north = halos(cells[:1])
    south_rest, north_rest = halos(cells[1:])
    first, local_pred = stencil_call(coeffs, cells[:1], south, north, obs_index)
    (rest,) = stencil_call(coeffs, cells[1:], south_rest, north_rest)
    transform = analysis_call(local_pred, weight, obs_value)
    piece = lax.all_gather(jnp.concatenate([first, rest], axis=0), "member", axis=0, tiled=False)
    blended = blend_call(transform, piece)
    return blended.transpose(2, 0, 1, 3)


def solution(mesh):
    return jax.shard_map(
        shards,
        mesh=mesh,
        in_specs=(
            P(("groups", "member"), None, "cell", None),
            P(),
            P("groups", None),
            P(("groups", "cell"), None),
            P(("groups", "cell")),
            P(("groups", "cell"), None),
            P(("groups", "cell"), None),
        ),
        out_specs=P(("groups", "member"), None, "cell", None),
        check_vma=False,
    )
```

time: 188 us -> 113 us (0.60)
  Pallas kernels: 0 us -> 66.5 us
  waiting for transfers between devices: 58.2 us -> 4.35 us
  matrix products: 43.5 us -> 0 us
  other arithmetic: 19.1 us -> 1.56 us
  blocking collectives: 16 us -> 0 us
  starting transfers between devices: 19.6 us -> 14.3 us
  between operations: 16.5 us -> 14.3 us
    pallas_call x0 -> x4, Pallas kernels: none -> 66.5 us  [the longest x1 47.6 us: analysis_call(): pl.pallas_call(functools.partial(analysis_kernel, n_cell, n_member), out_...]
    dot_general x82 -> x0, matrix products: 43.5 us -> none  [the longest x24 14.3 us: newton_step(): jnp.dot(upper, middle, precision=lax.Precision.HIGHEST, preferred_element...]
    ppermute x8 -> x4, waiting for transfers between devices: 35.5 us -> 0.81 us  [the longest x2 0.8 us: halos(): lax.ppermute(cells[:, rows - HALO:].astype(jnp.bfloat16), 'cell', up)]
    psum x1 -> x0, waiting for transfers between devices: 22.7 us -> none  [shards(): gram, gain = lax.psum((gram_part, gain_part), 'cell')]
    add x3 -> x0, other arithmetic: 10.5 us -> none  [stencil(): return result + diffusion * (north + south + east + west - 4.0 * centre)]
    psum x1 -> x0, blocking collectives: 8.64 us -> none  [shards(): gram, gain = lax.psum((gram_part, gain_part), 'cell')]
    all_gather x1 -> x0, blocking collectives: 7.35 us -> none  [shards(): predicted = lax.all_gather(local_pred, 'member', axis=0, tiled=True)]
    ppermute x8 -> x4, starting transfers between devices: 19.6 us -> 14.3 us  [the longest x2 11.6 us: halos(): lax.ppermute(cells[:, rows - HALO:].astype(jnp.bfloat16), 'cell', up)]
  transfers between devices with their start and end apart: 10 -> 5, of which waited for: 9 -> 2; matrix products, arithmetic and copies ran while one was open for 23% -> 3% of each run, Pallas kernels for 0% -> 48%
where the time goes in v1:
time: 113 us; the launch traced here: 112 us
  Pallas kernels  66.5 us (59%)
  starting transfers between devices  14.3 us (13%)
  between operations  14.3 us (13%)
  local copies, waits for them, and re-layouts  11.5 us (10%)
  waiting for transfers between devices  4.35 us (4%)
  other arithmetic  1.56 us (1%)
    pallas_call x1, Pallas kernels, analysis_call(): pl.pallas_call(functools.partial(analysis_kernel, n_cell, n_member), out_...  47.6 us
    pallas_call x2, Pallas kernels, stencil_call(): pl.pallas_call(functools.partial(stencil_kernel, chunk, with_obs), grid=(...  13.9 us
    ppermute x2, starting transfers between devices, halos(): lax.ppermute(cells[:, rows - HALO:].astype(jnp.bfloat16), 'cell', up)  11.6 us
    unnamed x14, local copies, waits for them, and re-layouts  5.85 us
    pallas_call x1, Pallas kernels, blend_call(): pl.pallas_call(blend_kernel, grid=(fields, rows // group), in_specs=[pl.B...  5.08 us
    all_gather x1, waiting for transfers between devices, shards(): lax.all_gather(jnp.concatenate([first, rest], axis=0), 'member', axis=0,...  3.52 us
    transpose x1, local copies, waits for them, and re-layouts, shards(): return blended.transpose(2, 0, 1, 3)  3.49 us
    ppermute x2, starting transfers between devices, halos(): north = lax.ppermute(cells[:, :HALO].astype(jnp.bfloat16), 'cell', down)  2.69 us
  transfers between devices with their start and end apart: 5, of which 2 were waited for; matrix products, arithmetic and copies ran while one was open for 3% of the time, Pallas kernels for 48%

profile of v1, /device:TPU:0, one launch (start us, length us, event | category | flops | bytes accessed | tf_op | source)
XLA Modules:
  0.0 112.5 jit_solution(3308068676399121284)
XLA Ops:
  6.5 0.0 all-gather.3.cloned.1.call-start
  6.5 3.6 %copy.33 = bf16[64,3,8,512]{3,0,2,1:T(8,128)(2,1)S(1)} copy(f32[64,3,8,512]{3,2,1,0:T(8,128)} %param.7) | data formatting | bytes 4718592 | tf_op args[0]
  10.1 0.0 copy-start.3
  10.1 0.0 copy-start.5
  10.1 0.0 copy-start.2
  10.1 0.8 fusion.2
  11.0 1.4 %collective-permute-start.1 = (bf16[1,4,64,512]{3,2,1,0:T(8,128)(2,1)}, bf16[1,4,64,512]{3,2,1,0:T(8,128)(2,1)S(1)}, u32[]{:S(2)}, u32[]{:S(2)}) collective-permute-start(bf16[1,4,64,512]{3,2,1,0:T(8,128)(2,1)} %get-tuple-element.11), channel_id=1, source_target_pairs={{4,0},{8,4},{12,8},{5,1},{9,5},{13,9},{6,2},{10,6},{14,10},{7,3},{... | collective-permute-start | bytes 786440 | tf_op jit(solution)/shard_map/ppermute | solution.py:328
  12.4 6.3 %collective-permute-start = (bf16[1,4,64,512]{3,2,1,0:T(8,128)(2,1)}, bf16[1,4,64,512]{3,2,1,0:T(8,128)(2,1)}, u32[]{:S(2)}, u32[]{:S(2)}) collective-permute-start(bf16[1,4,64,512]{3,2,1,0:T(8,128)(2,1)} %get-tuple-element.12), channel_id=1, source_target_pairs={{0,4},{4,8},{8,12},{1,5},{5,9},{9,13},{2,6},{6,10},{10,14},{3,7},{... | collective-permute-start | bytes 786440 | tf_op jit(solution)/shard_map/ppermute | solution.py:327
  18.7 1.1 fusion.1
  19.7 1.3 %collective-permute-start.3 = (bf16[2,4,64,512]{3,2,1,0:T(8,128)(2,1)}, bf16[2,4,64,512]{3,2,1,0:T(8,128)(2,1)}, u32[]{:S(2)}, u32[]{:S(2)}) collective-permute-start(bf16[2,4,64,512]{3,2,1,0:T(8,128)(2,1)} %get-tuple-element.9), channel_id=1, source_target_pairs={{4,0},{8,4},{12,8},{5,1},{9,5},{13,9},{6,2},{10,6},{14,10},{7,3},{... | collective-permute-start | bytes 1572872 | tf_op jit(solution)/shard_map/ppermute | solution.py:328
  21.0 5.3 %collective-permute-start.2 = (bf16[2,4,64,512]{3,2,1,0:T(8,128)(2,1)}, bf16[2,4,64,512]{3,2,1,0:T(8,128)(2,1)}, u32[]{:S(2)}, u32[]{:S(2)}) collective-permute-start(bf16[2,4,64,512]{3,2,1,0:T(8,128)(2,1)} %get-tuple-element.10), channel_id=1, source_target_pairs={{0,4},{4,8},{8,12},{1,5},{5,9},{9,13},{2,6},{6,10},{10,14},{3,7},{... | collective-permute-start | bytes 1572872 | tf_op jit(solution)/shard_map/ppermute | solution.py:327
  26.4 0.0 copy-done.3
  26.4 0.1 select_reduce_fusion.1
  26.5 0.0 copy-done.5
  26.5 0.1 select_reduce_fusion
  26.7 0.0 copy-done.2
  26.7 1.8 %copy.32 = f32[64,3,8,512]{3,0,2,1:T(8,128)S(1)} copy(f32[64,3,8,512]{3,2,1,0:T(8,128)S(1)} %copy-done.2) | data formatting | bytes 6291456 | tf_op args[0]
  28.5 0.1 slice.44.refs_1_
  28.6 0.0 copy-start
  28.6 0.2 slice.47.refs_0_
  28.8 0.0 collective-permute-done.1.refs_3_
  28.8 0.0 collective-permute-done.refs_2_
  28.8 0.4 copy-done
  29.3 6.4 %shard_map.73 = (bf16[1,8,64,512]{3,2,1,0:T(8,128)(2,1)S(1)}, f32[64,512]{1,0:T(8,128)S(1)}) custom-call(f32[20,16]{1,0:T(8,128)S(1)} %select_bitcast_fusion.coeff_ref, s32[1,512]{1,0:T(1,128)S(1)} %copy-done, f32[1,8,64,512]{3,2,1,0:T(8,128)S(1)} %slice.44.refs_1_, bf16[1,4,64,512]{3,2,1,0:T(8,128)(2,1)} %collective-permute-done.refs_2_, ...), custom_call_target="tpu_custom_call" | custom-call | flops 23592960 | bytes 2097152 | tf_op jit(solution)/shard_map/pallas_call | solution.py:116
  35.7 0.0 collective-permute-done.3.refs_2_
  35.7 0.8 collective-permute-done.2.refs_1_
  36.5 7.5 %shard_map.75 = bf16[2,8,64,512]{3,2,1,0:T(8,128)(2,1)S(1)} custom-call(f32[20,16]{1,0:T(8,128)S(1)} %select_bitcast_fusion.coeff_ref, f32[2,8,64,512]{3,2,1,0:T(8,128)S(1)} %slice.47.refs_0_, bf16[2,4,64,512]{3,2,1,0:T(8,128)(2,1)} %collective-permute-done.2.refs_1_, bf16[2,4,64,512]{3,2,1,0:T(8,128)(2,1)} %collective-permute-done.3.refs_2_), custom_call_target="tpu_custom_call" | custom-call | flops 47185920 | bytes 4194304 | tf_op jit(solution)/shard_map/pallas_call | solution.py:116
  44.0 1.3 %pad_maximum_fusion = bf16[3,8,64,512]{3,2,1,0:T(8,128)(2,1)} fusion(bf16[2,8,64,512]{3,2,1,0:T(8,128)(2,1)S(1)} %shard_map.75, bf16[1,8,64,512]{3,2,1,0:T(8,128)(2,1)S(1)} %get-tuple-element.8), kind=kLoop, calls=%fused_computation.1 | loop fusion | flops 786432 | bytes 3145728 | tf_op jit(solution)/shard_map/concatenate | solution.py:346
  45.2 0.0 copy-start.4
  45.3 0.0 copy-start.1
  45.3 0.0 all-gather.3.cloned.1.call-update
  45.9 0.0 copy-done.4
  46.0 0.0 copy-done.1
  46.0 47.6 %shard_map.74.coeff_ref = bf16[64,256]{1,0:T(8,128)(2,1)S(1)} custom-call(f32[64,512]{1,0:T(8,128)S(1)} %get-tuple-element.7.pred_ref, f32[1,512]{1,0:T(1,128)S(1)} %compare_select_fusion.weight_ref, f32[1,512]{1,0:T(1,128)S(1)} %copy-done.1), custom_call_target="tpu_custom_call" | custom-call | flops 14495514624 | bytes 1048576 | tf_op jit(solution)/shard_map/pallas_call | solution.py:270
  93.5 3.5 %all-gather.3.cloned.1.call-done = bf16[12,8,64,512]{3,2,1,0:T(8,128)(2,1)} async-done(((bf16[3,8,64,512]{3,2,1,0:T(8,128)(2,1)}), bf16[12,8,64,512]{3,2,1,0:T(8,128)(2,1)}) %all-gather.3.cloned.1.call-update) | async-done | bytes 6291472 | tf_op jit(solution)/shard_map/all_gather | solution.py:346
  97.1 5.1 %shard_map.76 = f32[3,8,64,512]{3,2,1,0:T(8,128)S(1)} custom-call(bf16[64,256]{1,0:T(8,128)(2,1)S(1)} %shard_map.74.coeff_ref, bf16[4,3,8,64,512]{4,3,2,1,0:T(8,128)(2,1)} %bitcast.19), custom_call_target="tpu_custom_call" | custom-call | tf_op jit(solution)/shard_map/pallas_call | solution.py:309
  102.1 3.5 %copy.26 = f32[64,3,8,512]{3,2,1,0:T(8,128)} copy(f32[64,3,8,512]{3,0,2,1:T(8,128)S(1)} %bitcast.16) | data formatting | bytes 6291456 | tf_op jit(solution)/shard_map/transpose | solution.py:348
  (14 shorter events, 0.1 us)
Async XLA Ops:
  6.5 90.5 %all-gather.3.cloned.1.call-start = ((), (), s32[]{:S(2)}) async-start(), calls=%async_computation | async-start | bytes 7864320 | tf_op jit(solution)/shard_map/all_gather | solution.py:346
  10.1 16.3 %copy-start.3 = (s32[8,4]{0,1:T(4,128)S(1)}, s32[8,4]{0,1:T(4,128)}, u32[]{:S(2)}) copy-start(s32[8,4]{0,1:T(4,128)} %param.9) | copy-start | bytes 388
  10.1 16.4 %copy-start.5 = (f32[8,2]{0,1:T(2,128)S(1)}, f32[8,2]{0,1:T(2,128)}, u32[]{:S(2)}) copy-start(f32[8,2]{0,1:T(2,128)} %param.8) | copy-start | bytes 196
  10.1 16.6 %copy-start.2 = (f32[64,3,8,512]{3,2,1,0:T(8,128)S(1)}, f32[64,3,8,512]{3,2,1,0:T(8,128)}, u32[]{:S(2)}) copy-start(f32[64,3,8,512]{3,2,1,0:T(8,128)} %param.7) | copy-start | bytes 9437188
  11.0 17.8 %collective-permute-start.1 = (bf16[1,4,64,512]{3,2,1,0:T(8,128)(2,1)}, bf16[1,4,64,512]{3,2,1,0:T(8,128)(2,1)S(1)}, u32[]{:S(2)}, u32[]{:S(2)}) collective-permute-start(bf16[1,4,64,512]{3,2,1,0:T(8,128)(2,1)} %get-tuple-element.11), channel_id=1, source_target_pairs={{4,0},{8,4},{12,8},{5,1},{9,5},{13,9},{6,2},{10,6},{14,10},{7,3},{... | collective-permute-start | bytes 786440 | tf_op jit(solution)/shard_map/ppermute | solution.py:328
  12.4 16.4 %collective-permute-start = (bf16[1,4,64,512]{3,2,1,0:T(8,128)(2,1)}, bf16[1,4,64,512]{3,2,1,0:T(8,128)(2,1)}, u32[]{:S(2)}, u32[]{:S(2)}) collective-permute-start(bf16[1,4,64,512]{3,2,1,0:T(8,128)(2,1)} %get-tuple-element.12), channel_id=1, source_target_pairs={{0,4},{4,8},{8,12},{1,5},{5,9},{9,13},{2,6},{6,10},{10,14},{3,7},{... | collective-permute-start | bytes 786440 | tf_op jit(solution)/shard_map/ppermute | solution.py:327
  19.7 16.0 %collective-permute-start.3 = (bf16[2,4,64,512]{3,2,1,0:T(8,128)(2,1)}, bf16[2,4,64,512]{3,2,1,0:T(8,128)(2,1)}, u32[]{:S(2)}, u32[]{:S(2)}) collective-permute-start(bf16[2,4,64,512]{3,2,1,0:T(8,128)(2,1)} %get-tuple-element.9), channel_id=1, source_target_pairs={{4,0},{8,4},{12,8},{5,1},{9,5},{13,9},{6,2},{10,6},{14,10},{7,3},{... | collective-permute-start | bytes 1572872 | tf_op jit(solution)/shard_map/ppermute | solution.py:328
  21.0 15.5 %collective-permute-start.2 = (bf16[2,4,64,512]{3,2,1,0:T(8,128)(2,1)}, bf16[2,4,64,512]{3,2,1,0:T(8,128)(2,1)}, u32[]{:S(2)}, u32[]{:S(2)}) collective-permute-start(bf16[2,4,64,512]{3,2,1,0:T(8,128)(2,1)} %get-tuple-element.10), channel_id=1, source_target_pairs={{0,4},{4,8},{8,12},{1,5},{5,9},{9,13},{2,6},{6,10},{10,14},{3,7},{... | collective-permute-start | bytes 1572872 | tf_op jit(solution)/shard_map/ppermute | solution.py:327
  28.6 0.7 copy-start
  45.2 0.7 copy-start.4
  45.3 0.7 copy-start.1
Sparse Core Ops, SparseCore 0:
  45.4 51.6 all-gather.2

commit v2 on v1

v2 whole, which is shorter than its diff:
```python
import functools

import jax
import jax.numpy as jnp
from jax import lax
from jax.experimental import pallas as pl
from jax.experimental.pallas import tpu as pltpu
from jax.sharding import PartitionSpec as P

SUBSTEPS = 4
BAND = 4
ROOT_STEPS = 24
HALO = SUBSTEPS
DIFFUSION = 0.02
MESH = pl.DeviceIdType.MESH
HIGHEST = lax.Precision.HIGHEST
VMEM_LIMIT = 48 * 1024 * 1024


def stencil_coeffs(regimes, wind_table, first_row, tile_rows, row_total):
    row_ids = first_row - HALO + jnp.arange(tile_rows + 2 * HALO)
    band_ids = jnp.clip(row_ids, 0, row_total - 1) // BAND
    band_hits = band_ids[:, None, None] == jnp.arange(regimes.shape[0])[None, :, None]
    ids = jnp.sum(jnp.where(band_hits, regimes[None], 0), axis=1)
    hits = ids[:, :, None, None] == jnp.arange(wind_table.shape[0])[None, None, :, None]
    speed = jnp.sum(jnp.where(hits, wind_table[None, None], 0.0), axis=2)
    cx, cy = speed[:, :, 0], speed[:, :, 1]
    parts = [
        1.0 - jnp.abs(cx) - jnp.abs(cy) - 4.0 * DIFFUSION,
        jnp.maximum(cx, 0.0) + DIFFUSION,
        DIFFUSION - jnp.minimum(cx, 0.0),
        jnp.maximum(cy, 0.0) + DIFFUSION,
        DIFFUSION - jnp.minimum(cy, 0.0),
    ]
    inside = (row_ids >= 0) & (row_ids < row_total)
    table = jnp.where(inside[:, None, None], jnp.stack(parts, axis=2), 0.0)
    return table.reshape(row_ids.shape[0], SUBSTEPS * 5).T


def stencil_kernel(
    n_cell,
    chunk,
    coeff_ref,
    index_ref,
    x_ref,
    out_ref,
    pred_ref,
    keep,
    edge_up,
    edge_down,
    south,
    north,
    send_up,
    recv_up,
    send_down,
    recv_down,
):
    cell = lax.axis_index("cell")
    fields, rows, members, width = x_ref.shape
    has_south, has_north = cell > 0, cell < n_cell - 1
    below = lax.rem(cell + n_cell - 1, n_cell)
    above = lax.rem(cell + 1, n_cell)

    barrier = pltpu.get_barrier_semaphore()

    @pl.when(has_south)
    def _():
        pl.semaphore_signal(barrier, inc=1, device_id={"cell": below}, device_id_type=MESH)

    @pl.when(has_north)
    def _():
        pl.semaphore_signal(barrier, inc=1, device_id={"cell": above}, device_id_type=MESH)

    for f in range(fields):
        edge_up[f] = x_ref[f, rows - HALO :].astype(jnp.bfloat16)
        edge_down[f] = x_ref[f, :HALO].astype(jnp.bfloat16)

    neighbours = jnp.where(has_south, 1, 0) + jnp.where(has_north, 1, 0)
    pl.semaphore_wait(barrier, neighbours)

    def upward(f):
        return pltpu.make_async_remote_copy(
            src_ref=edge_up.at[f],
            dst_ref=south.at[f],
            send_sem=send_up.at[f],
            recv_sem=recv_up.at[f],
            device_id={"cell": above},
            device_id_type=MESH,
        )

    def downward(f):
        return pltpu.make_async_remote_copy(
            src_ref=edge_down.at[f],
            dst_ref=north.at[f],
            send_sem=send_down.at[f],
            recv_sem=recv_down.at[f],
            device_id={"cell": below},
            device_id_type=MESH,
        )

    for f in range(fields):

        @pl.when(has_north)
        def _():
            upward(f).start()

        @pl.when(has_south)
        def _():
            downward(f).start()

    @pl.when(cell == 0)
    def _():
        south[...] = jnp.zeros_like(south)

    @pl.when(cell == n_cell - 1)
    def _():
        north[...] = jnp.zeros_like(north)

    lane = lax.broadcasted_iota(jnp.int32, (chunk, width), 1)
    slots = index_ref.shape[1]
    column = lax.broadcasted_iota(jnp.int32, (width, slots), 0)

    def one_field(f, outer):
        @pl.when(has_south)
        def _():
            upward(f).wait_recv()

        @pl.when(has_north)
        def _():
            downward(f).wait_recv()

        def one_chunk(step_at, carry):
            at = pl.ds(pl.multiple_of(step_at * chunk, chunk), chunk)
            cells = [south[f, i, at, :].astype(jnp.float32) for i in range(HALO)]
            cells += [x_ref[f, i, at, :] for i in range(rows)]
            cells += [north[f, i, at, :].astype(jnp.float32) for i in range(HALO)]
            for s in range(SUBSTEPS):
                fresh = list(cells)
                for i in range(s + 1, rows + 2 * HALO - s - 1):
                    q = cells[i]
                    west = jnp.where(lane == 0, 0.0, pltpu.roll(q, 1, 1))
                    east = jnp.where(lane == width - 1, 0.0, pltpu.roll(q, width - 1, 1))
                    fresh[i] = (
                        q * coeff_ref[s * 5, i]
                        + cells[i - 1] * coeff_ref[s * 5 + 1, i]
                        + cells[i + 1] * coeff_ref[s * 5 + 2, i]
                        + west * coeff_ref[s * 5 + 3, i]
                        + east * coeff_ref[s * 5 + 4, i]
                    )
                cells = fresh
            for i in range(rows):
                out_ref[f, i, at, :] = cells[HALO + i].astype(jnp.bfloat16)
                keep[i, at, :] = cells[HALO + i]
            return carry

        lax.fori_loop(0, members // chunk, one_chunk, 0)

        @pl.when(f == 0)
        def _():
            pred_ref[...] = jnp.zeros_like(pred_ref)

            def one_row(i, carry):
                hits = jnp.where(column == index_ref[...] - i * width, 1.0, 0.0)
                picked = jnp.dot(
                    jnp.concatenate(split3(keep[i]), axis=0),
                    hits.astype(jnp.bfloat16),
                    preferred_element_type=jnp.float32,
                )
                pred_ref[...] += (
                    picked[:members] + picked[members : 2 * members] + picked[2 * members :]
                )
                return carry

            lax.fori_loop(0, rows, one_row, 0)

        return outer

    lax.fori_loop(0, fields, one_field, 0)

    for f in range(fields):

        @pl.when(has_north)
        def _():
            upward(f).wait_send()

        @pl.when(has_south)
        def _():
            downward(f).wait_send()


def stencil_call(coeffs, obs_index, cells):
    fields, rows, members, width = cells.shape
    vmem = pl.BlockSpec(memory_space=pltpu.VMEM)
    edge = pltpu.VMEM((fields, HALO, members, width), jnp.bfloat16)
    return pl.pallas_call(
        functools.partial(stencil_kernel, lax.axis_size("cell"), 16),
        in_specs=[pl.BlockSpec(memory_space=pltpu.SMEM), vmem, vmem],
        out_specs=[vmem, vmem],
        out_shape=[
            jax.ShapeDtypeStruct(cells.shape, jnp.bfloat16),
            jax.ShapeDtypeStruct((members, obs_index.shape[1]), jnp.float32),
        ],
        scratch_shapes=[pltpu.VMEM((rows, members, width), jnp.float32)]
        + [edge] * 4
        + [pltpu.SemaphoreType.DMA((fields,))] * 4,
        compiler_params=pltpu.CompilerParams(
            collective_id=1, has_side_effects=True, vmem_limit_bytes=VMEM_LIMIT
        ),
    )(coeffs, obs_index, cells)


def split3(x):
    high = x.astype(jnp.bfloat16)
    rest = x - high.astype(jnp.float32)
    middle = rest.astype(jnp.bfloat16)
    return high, middle, (rest - middle.astype(jnp.float32)).astype(jnp.bfloat16)


def six_products(a, b):
    left = jnp.concatenate([a[2], a[1], a[0], a[1], a[0], a[0]], axis=1)
    right = jnp.concatenate([b[0], b[1], b[2], b[0], b[1], b[0]], axis=0)
    return jnp.dot(left, right, preferred_element_type=jnp.float32)


def nt_dot(a, b):
    return lax.dot_general(
        a, b, (((1,), (1,)), ((), ())), precision=HIGHEST, preferred_element_type=jnp.float32
    )


def nn_dot(a, b):
    return jnp.dot(a, b, precision=HIGHEST, preferred_element_type=jnp.float32)


def analysis_kernel(
    n_cell,
    n_member,
    pred_ref,
    weight_ref,
    value_ref,
    forecast_ref,
    out_ref,
    pieces,
    coeff,
    everyone,
    mine,
    others,
    total,
    gram,
    upper,
    lower,
    send_pred,
    recv_pred,
    send_part,
    recv_part,
    send_gram,
    recv_gram,
    send_far,
    recv_far,
    send_mate,
    recv_mate,
):
    cell = lax.axis_index("cell")
    member = lax.axis_index("member")
    count = pred_ref.shape[0]
    members = count * n_member

    barrier = pltpu.get_barrier_semaphore()
    for d in range(1, n_member):
        pl.semaphore_signal(
            barrier, inc=1, device_id={"member": lax.rem(member + d, n_member)}, device_id_type=MESH
        )
    for d in range(1, n_cell):
        pl.semaphore_signal(
            barrier, inc=1, device_id={"cell": lax.rem(cell + d, n_cell)}, device_id_type=MESH
        )
    pl.semaphore_wait(barrier, n_member + n_cell - 2)

    own = pl.ds(pl.multiple_of(member * count, count), count)
    fields, rows_here = forecast_ref.shape[:2]
    chips = n_member // 2
    mate = member + 1 - 2 * lax.rem(member, 2)

    def to_far(d, f):
        return pltpu.make_async_remote_copy(
            src_ref=forecast_ref.at[f],
            dst_ref=pieces.at[member, f],
            send_sem=send_far.at[d, f],
            recv_sem=recv_far.at[d, f],
            device_id={"member": lax.rem(member + 2 * d, n_member)},
            device_id_type=MESH,
        )

    def to_mate(d, f):
        owner = lax.rem(member + n_member - 2 * d, n_member)
        return pltpu.make_async_remote_copy(
            src_ref=forecast_ref.at[f] if d == 0 else pieces.at[owner, f],
            dst_ref=pieces.at[owner, f],
            send_sem=send_mate.at[d, f],
            recv_sem=recv_mate.at[d, f],
            device_id={"member": mate},
            device_id_type=MESH,
        )

    def send_field(f):
        for d in range(1, chips):
            to_far(d, f).start()
        to_mate(0, f).start()

    def forward_field(f):
        for d in range(1, chips):
            to_far(d, f).wait_recv()
            to_mate(d, f).start()

    copies = []
    for d in range(1, n_member):
        copy = pltpu.make_async_remote_copy(
            src_ref=pred_ref,
            dst_ref=everyone.at[own],
            send_sem=send_pred.at[d],
            recv_sem=recv_pred.at[d],
            device_id={"member": lax.rem(member + d, n_member)},
            device_id_type=MESH,
        )
        copy.start()
        copies.append(copy)
    everyone[own, :] = pred_ref[...]
    for copy in copies:
        copy.wait()

    send_field(0)
    predicted = everyone[...]
    ybar = jnp.mean(predicted, axis=0, keepdims=True)
    weight = weight_ref[...]
    scaled = (predicted - ybar) * weight
    local = (pred_ref[...] - ybar) * weight
    innovation = jnp.broadcast_to(weight * (value_ref[...] - ybar), (8, weight.shape[1]))
    mine[...] = nt_dot(jnp.concatenate([local, innovation], axis=0), scaled)

    copies = []
    for d in range(1, n_cell):
        copy = pltpu.make_async_remote_copy(
            src_ref=mine,
            dst_ref=others.at[d - 1],
            send_sem=send_part.at[d],
            recv_sem=recv_part.at[d],
            device_id={"cell": lax.rem(cell + d, n_cell)},
            device_id_type=MESH,
        )
        copy.start()
        copies.append(copy)
    for copy in copies:
        copy.wait()
    summed = mine[...]
    for d in range(n_cell - 1):
        summed = summed + others[d]
    total[...] = summed

    copies = []
    for d in range(1, n_member):
        copy = pltpu.make_async_remote_copy(
            src_ref=total.at[pl.ds(0, count)],
            dst_ref=gram.at[own],
            send_sem=send_gram.at[d],
            recv_sem=recv_gram.at[d],
            device_id={"member": lax.rem(member + d, n_member)},
            device_id_type=MESH,
        )
        copy.start()
        copies.append(copy)
    gram[own, :] = total[pl.ds(0, count), :]
    for copy in copies:
        copy.wait()

    for f in range(1, fields):
        send_field(f)
    pieces[member] = forecast_ref[...]

    rows = lax.broadcasted_iota(jnp.int32, (members, members), 0)
    columns = lax.broadcasted_iota(jnp.int32, (members, members), 1)
    identity = jnp.where(rows == columns, 1.0, 0.0).astype(jnp.float32)
    precision = gram[...] + (members - 1.0) * identity
    scale = jnp.sum(jnp.sum(precision * identity, axis=1, keepdims=True), axis=0, keepdims=True)
    upper[...] = precision / scale
    lower[...] = identity

    def newton(step, carry):
        y, z = split3(upper[...]), split3(lower[...])
        middle = split3(1.5 * identity - 0.5 * six_products(z, y))
        upper[...] = six_products(y, middle)
        lower[...] = six_products(middle, z)
        return carry

    for f in range(fields):
        lax.fori_loop(ROOT_STEPS * f // fields, ROOT_STEPS * (f + 1) // fields, newton, 0)
        forward_field(f)

    gain = total[pl.ds(count, 8), :]
    half_way = nt_dot(gain, lower[...])
    mean_weights = nt_dot(half_way, lower[...])[0:1, :] / scale
    root = jnp.sqrt((members - 1.0) / scale) * lower[own, :]
    blend = mean_weights + root
    transform = blend - jnp.mean(blend, axis=1, keepdims=True) + 1.0 / members
    coeff[...] = transform.astype(jnp.bfloat16)

    for f in range(fields):
        for d in range(chips):
            to_mate(d, f).wait()
        for d in range(1, chips):
            to_far(d, f).wait_send()

        def blend_row(r, carry):
            block = pieces[:, f, r].reshape(members, pieces.shape[4])
            out_ref[f, r] = jnp.dot(coeff[...], block, preferred_element_type=jnp.float32)
            return carry

        lax.fori_loop(0, rows_here, blend_row, 0)


def analysis_call(local_pred, weight, value, forecast):
    n_cell, n_member = lax.axis_size("cell"), lax.axis_size("member")
    count, slots = local_pred.shape
    members = count * n_member
    fields = forecast.shape[0]
    vmem = pl.BlockSpec(memory_space=pltpu.VMEM)
    dma = pltpu.SemaphoreType.DMA
    return pl.pallas_call(
        functools.partial(analysis_kernel, n_cell, n_member),
        out_shape=jax.ShapeDtypeStruct(forecast.shape, jnp.float32),
        in_specs=[vmem] * 4,
        out_specs=vmem,
        scratch_shapes=[
            pltpu.VMEM((n_member,) + forecast.shape, jnp.bfloat16),
            pltpu.VMEM((count, members), jnp.bfloat16),
            pltpu.VMEM((members, slots), jnp.float32),
            pltpu.VMEM((count + 8, members), jnp.float32),
            pltpu.VMEM((n_cell - 1, count + 8, members), jnp.float32),
            pltpu.VMEM((count + 8, members), jnp.float32),
            pltpu.VMEM((members, members), jnp.float32),
            pltpu.VMEM((members, members), jnp.float32),
            pltpu.VMEM((members, members), jnp.float32),
            dma((n_member,)),
            dma((n_member,)),
            dma((n_cell,)),
            dma((n_cell,)),
            dma((n_member,)),
            dma((n_member,)),
        ]
        + [dma((n_member // 2, fields))] * 4,
        compiler_params=pltpu.CompilerParams(
            collective_id=0, has_side_effects=True, vmem_limit_bytes=VMEM_LIMIT
        ),
    )(local_pred, weight, value, forecast)


def shards(prior_sample_set, wind_table, regimes, obs_index, obs_count, obs_value, obs_var):
    tile_rows = prior_sample_set.shape[2]
    row_total = tile_rows * lax.axis_size("cell")
    first_row = lax.axis_index("cell") * tile_rows
    coeffs = stencil_coeffs(regimes, wind_table, first_row, tile_rows, row_total)
    live = jnp.arange(obs_var.shape[1])[None, :] < obs_count[0]
    weight = live.astype(jnp.float32) / jnp.sqrt(obs_var)

    cells = prior_sample_set.transpose(1, 2, 0, 3)
    forecast, local_pred = stencil_call(coeffs, obs_index, cells)
    blended = analysis_call(local_pred, weight, obs_value, forecast)
    return blended.transpose(2, 0, 1, 3)


def solution(mesh):
    return jax.shard_map(
        shards,
        mesh=mesh,
        in_specs=(
            P(("groups", "member"), None, "cell", None),
            P(),
            P("groups", None),
            P(("groups", "cell"), None),
            P(("groups", "cell")),
            P(("groups", "cell"), None),
            P(("groups", "cell"), None),
        ),
        out_specs=P(("groups", "member"), None, "cell", None),
        check_vma=False,
    )
```

time: 113 us -> 90.4 us (0.80)
  starting transfers between devices: 14.3 us -> 0 us
  between operations: 14.3 us -> 0.77 us
  Pallas kernels: 66.5 us -> 79.9 us
  waiting for transfers between devices: 4.35 us -> 0 us
  local copies, waits for them, and re-layouts: 11.5 us -> 7.24 us
    ppermute x4 -> x0, starting transfers between devices: 14.3 us -> none  [the longest x2 11.6 us: halos(): lax.ppermute(cells[:, rows - HALO:].astype(jnp.bfloat16), 'cell', up)]
    pallas_call x3 -> x1, Pallas kernels: 18.9 us -> 26 us  [stencil_call(): pl.pallas_call(functools.partial(stencil_kernel, lax.axis_size('cell'), 1...]
    pallas_call x1, Pallas kernels: 47.6 us -> 53.9 us  [analysis_call(): pl.pallas_call(functools.partial(analysis_kernel, n_cell, n_member), out_...]
    all_gather x1 -> x0, waiting for transfers between devices: 3.52 us -> none  [shards(): lax.all_gather(jnp.concatenate([first, rest], axis=0), 'member', axis=0,...]
    slice x4 -> x0, local copies, waits for them, and re-layouts: 2.15 us -> none  [the longest x2 1.91 us: halos(): north = lax.ppermute(cells[:, :HALO].astype(jnp.bfloat16), 'cell', down)]
    unnamed x14 -> x5, local copies, waits for them, and re-layouts: 5.85 us -> 3.73 us
    concatenate x1 -> x0, other arithmetic: 1.28 us -> none  [shards(): jnp.concatenate([first, rest], axis=0)]
  transfers between devices with their start and end apart: 5 -> 0, of which waited for: 2 -> 0; matrix products, arithmetic and copies ran while one was open for 3% -> 0% of each run, Pallas kernels for 48% -> 0%
where the time goes in v2:
time: 90.4 us; the launch traced here: 90.2 us
  Pallas kernels  79.9 us (88%)
  local copies, waits for them, and re-layouts  7.24 us (8%)
  other arithmetic  2.32 us (3%)
    pallas_call x1, Pallas kernels, analysis_call(): pl.pallas_call(functools.partial(analysis_kernel, n_cell, n_member), out_...  53.9 us
    pallas_call x1, Pallas kernels, stencil_call(): pl.pallas_call(functools.partial(stencil_kernel, lax.axis_size('cell'), 1...  26 us
    unnamed x5, local copies, waits for them, and re-layouts  3.73 us
    transpose x1, local copies, waits for them, and re-layouts, shards(): return blended.transpose(2, 0, 1, 3)  3.49 us

profile of v2, /device:TPU:0, one launch (start us, length us, event | category | flops | bytes accessed | tf_op | source)
XLA Modules:
  0.0 90.2 jit_solution(13644800425036605166)
XLA Ops:
  0.7 0.8 select_reduce_fusion.1
  1.5 0.7 compare_select_fusion.weight_ref
  2.2 0.8 select_reduce_fusion
  3.1 0.0 copy-start.1
  3.1 3.7 %copy.26 = f32[64,3,8,512]{3,0,2,1:T(8,128)S(1)} copy(f32[64,3,8,512]{3,2,1,0:T(8,128)} %param.7) | data formatting | bytes 6291456 | tf_op args[0]
  6.8 0.0 copy-start
  6.8 0.0 copy-done.1
  6.8 26.0 %shard_map.73 = (bf16[3,8,64,512]{3,2,1,0:T(8,128)(2,1)S(1)}, f32[64,512]{1,0:T(8,128)S(1)}) custom-call(f32[20,16]{1,0:T(8,128)S(1)} %select_bitcast_fusion.coeff_ref, s32[1,512]{1,0:T(1,128)S(1)} %copy-done.1, f32[3,8,64,512]{3,2,1,0:T(8,128)S(1)} %bitcast.12), custom_call_target="tpu_custom_call" | custom-call | tf_op jit(solution)/shard_map/pallas_call | solution.py:195
  32.8 0.0 copy-done
  32.8 53.9 %shard_map.74 = f32[3,8,64,512]{3,2,1,0:T(8,128)S(1)} custom-call(f32[64,512]{1,0:T(8,128)S(1)} %get-tuple-element.7.pred_ref, f32[1,512]{1,0:T(1,128)S(1)} %compare_select_fusion.weight_ref, f32[1,512]{1,0:T(1,128)S(1)} %copy-done, bf16[3,8,64,512]{3,2,1,0:T(8,128)(2,1)S(1)} %get-tuple-element.8.forecast_ref), custom_call_target="tpu_custom_call" | custom-call | tf_op jit(solution)/shard_map/pallas_call | solution.py:427
  86.7 3.5 %copy.22 = f32[64,3,8,512]{3,2,1,0:T(8,128)} copy(f32[64,3,8,512]{3,0,2,1:T(8,128)S(1)} %bitcast.13) | data formatting | bytes 6291456 | tf_op jit(solution)/shard_map/transpose | solution.py:467
  (13 shorter events, 0.1 us)
Async XLA Ops:
  3.1 3.7 %copy-start.1 = (s32[1,512]{1,0:T(1,128)S(1)}, s32[1,512]{1,0:T(1,128)}, u32[]{:S(2)}) copy-start(s32[1,512]{1,0:T(1,128)} %index_ref.1) | copy-start | bytes 6148
  6.8 26.0 %copy-start = (f32[1,512]{1,0:T(1,128)S(1)}, f32[1,512]{1,0:T(1,128)}, u32[]{:S(2)}) copy-start(f32[1,512]{1,0:T(1,128)} %value_ref.1) | copy-start | bytes 6148

commit v3 on v0

v3 whole, which is shorter than its diff:
```python
import functools

import jax
import jax.numpy as jnp
from jax import lax
from jax.experimental import pallas as pl
from jax.experimental.pallas import tpu as pltpu
from jax.sharding import PartitionSpec as P

SUBSTEPS = 4
BAND = 4
ROOT_STEPS = 24
HALO = SUBSTEPS
DIFFUSION = 0.02
MESH = pl.DeviceIdType.MESH
HIGHEST = lax.Precision.HIGHEST
VMEM_LIMIT = 56 * 1024 * 1024
CHUNK = 16


def split3(x):
    high = x.astype(jnp.bfloat16)
    rest = x - high.astype(jnp.float32)
    middle = rest.astype(jnp.bfloat16)
    return high, middle, (rest - middle.astype(jnp.float32)).astype(jnp.bfloat16)


def six_products(a, b):
    left = jnp.concatenate([a[2], a[1], a[0], a[1], a[0], a[0]], axis=1)
    right = jnp.concatenate([b[0], b[1], b[2], b[0], b[1], b[0]], axis=0)
    return jnp.dot(left, right, preferred_element_type=jnp.float32)


def nt_dot(a, b):
    return lax.dot_general(
        a, b, (((1,), (1,)), ((), ())), precision=HIGHEST, preferred_element_type=jnp.float32
    )


def nn_dot(a, b):
    return jnp.dot(a, b, precision=HIGHEST, preferred_element_type=jnp.float32)


def cycle_kernel(
    n_cell,
    n_member,
    regime_ref,
    wind_ref,
    count_ref,
    index_ref,
    value_ref,
    var_ref,
    x_ref,
    out_ref,
    table,
    keep,
    edge_up,
    edge_down,
    south,
    north,
    forecast,
    pieces,
    pred,
    coeff,
    everyone,
    mine,
    others,
    total,
    gram,
    upper,
    lower,
    send_up,
    recv_up,
    send_down,
    recv_down,
    send_pred,
    recv_pred,
    send_part,
    recv_part,
    send_gram,
    recv_gram,
    send_far,
    recv_far,
    send_mate,
    recv_mate,
):
    cell = lax.axis_index("cell")
    member = lax.axis_index("member")
    fields, rows, count, width = x_ref.shape
    slots = index_ref.shape[1]
    members = count * n_member
    chips = n_member // 2
    mate = member + 1 - 2 * lax.rem(member, 2)
    own = pl.ds(pl.multiple_of(member * count, count), count)
    has_south, has_north = cell > 0, cell < n_cell - 1

    barrier = pltpu.get_barrier_semaphore()
    for d in range(1, n_member):
        pl.semaphore_signal(
            barrier, inc=1, device_id={"member": lax.rem(member + d, n_member)}, device_id_type=MESH
        )
    for d in range(1, n_cell):
        pl.semaphore_signal(
            barrier, inc=1, device_id={"cell": lax.rem(cell + d, n_cell)}, device_id_type=MESH
        )

    def remote(src, dst, send, recv, **device):
        return pltpu.make_async_remote_copy(
            src_ref=src,
            dst_ref=dst,
            send_sem=send,
            recv_sem=recv,
            device_id=device,
            device_id_type=MESH,
        )

    def upward(f):
        above = lax.rem(cell + 1, n_cell)
        return remote(edge_up.at[f], south.at[f], send_up.at[f], recv_up.at[f], cell=above)

    def downward(f):
        below = lax.rem(cell + n_cell - 1, n_cell)
        return remote(edge_down.at[f], north.at[f], send_down.at[f], recv_down.at[f], cell=below)

    def to_far(d, f):
        return remote(
            forecast.at[f],
            pieces.at[member, f],
            send_far.at[d, f],
            recv_far.at[d, f],
            member=lax.rem(member + 2 * d, n_member),
        )

    def to_mate(d, f):
        owner = lax.rem(member + n_member - 2 * d, n_member)
        return remote(
            forecast.at[f] if d == 0 else pieces.at[owner, f],
            pieces.at[owner, f],
            send_mate.at[d, f],
            recv_mate.at[d, f],
            member=mate,
        )

    def send_field(f):
        for d in range(1, chips):
            to_far(d, f).start()
        to_mate(0, f).start()

    def forward_field(f):
        for d in range(1, chips):
            to_far(d, f).wait_recv()
            to_mate(d, f).start()

    def cast_edges(f):
        for i in range(HALO):
            edge_up[f, i] = x_ref[f, rows - HALO + i].astype(jnp.bfloat16)
            edge_down[f, i] = x_ref[f, i].astype(jnp.bfloat16)

    def send_edges(f):
        @pl.when(has_north)
        def _():
            upward(f).start()

        @pl.when(has_south)
        def _():
            downward(f).start()

    cast_edges(0)
    pl.semaphore_wait(barrier, n_member + n_cell - 2)
    send_edges(0)
    for f in range(1, fields):
        cast_edges(f)
        send_edges(f)

    @pl.when(cell == 0)
    def _():
        south[...] = jnp.zeros_like(south)

    @pl.when(cell == n_cell - 1)
    def _():
        north[...] = jnp.zeros_like(north)

    row_total = rows * n_cell

    def one_table_row(i, carry):
        row = cell * rows + i - HALO
        inside = jnp.where((row >= 0) & (row < row_total), 1.0, 0.0)
        band = jnp.minimum(jnp.maximum(row, 0), row_total - 1) // BAND
        for s in range(SUBSTEPS):
            regime = regime_ref[band, s]
            cx, cy = wind_ref[regime, 0], wind_ref[regime, 1]
            x_up, x_down = jnp.maximum(cx, 0.0), jnp.minimum(cx, 0.0)
            y_up, y_down = jnp.maximum(cy, 0.0), jnp.minimum(cy, 0.0)
            table[s * 5, i] = inside * (1.0 - 4.0 * DIFFUSION - x_up + x_down - y_up + y_down)
            table[s * 5 + 1, i] = inside * (x_up + DIFFUSION)
            table[s * 5 + 2, i] = inside * (DIFFUSION - x_down)
            table[s * 5 + 3, i] = inside * (y_up + DIFFUSION)
            table[s * 5 + 4, i] = inside * (DIFFUSION - y_down)
        return carry

    lax.fori_loop(0, rows + 2 * HALO, one_table_row, 0)

    lane = lax.broadcasted_iota(jnp.int32, (CHUNK, width), 1)

    def stencil(f):
        @pl.when(has_south)
        def _():
            upward(f).wait_recv()

        @pl.when(has_north)
        def _():
            downward(f).wait_recv()

        def one_chunk(step_at, carry):
            at = pl.ds(pl.multiple_of(step_at * CHUNK, CHUNK), CHUNK)
            cells = [south[f, i, at, :].astype(jnp.float32) for i in range(HALO)]
            cells += [x_ref[f, i, at, :] for i in range(rows)]
            cells += [north[f, i, at, :].astype(jnp.float32) for i in range(HALO)]
            for s in range(SUBSTEPS):
                fresh = list(cells)
                for i in range(s + 1, rows + 2 * HALO - s - 1):
                    q = cells[i]
                    west = jnp.where(lane == 0, 0.0, pltpu.roll(q, 1, 1))
                    east = jnp.where(lane == width - 1, 0.0, pltpu.roll(q, width - 1, 1))
                    fresh[i] = (
                        q * table[s * 5, i]
                        + cells[i - 1] * table[s * 5 + 1, i]
                        + cells[i + 1] * table[s * 5 + 2, i]
                        + west * table[s * 5 + 3, i]
                        + east * table[s * 5 + 4, i]
                    )
                cells = fresh
            for i in range(rows):
                forecast[f, i, at, :] = cells[HALO + i].astype(jnp.bfloat16)
                if f == 0:
                    keep[i, at, :] = cells[HALO + i]
            return carry

        lax.fori_loop(0, count // CHUNK, one_chunk, 0)

    stencil(0)
    column = lax.broadcasted_iota(jnp.int32, (width, slots), 0)
    pred[...] = jnp.zeros_like(pred)

    def pick_row(i, carry):
        hits = jnp.where(column == index_ref[...] - i * width, 1.0, 0.0)
        picked = jnp.dot(
            jnp.concatenate(split3(keep[i]), axis=0),
            hits.astype(jnp.bfloat16),
            preferred_element_type=jnp.float32,
        )
        pred[...] += picked[:count] + picked[count : 2 * count] + picked[2 * count :]
        return carry

    lax.fori_loop(0, rows, pick_row, 0)

    def share_pred(d):
        peer = lax.rem(member + d, n_member)
        return remote(pred, everyone.at[own], send_pred.at[d], recv_pred.at[d], member=peer)

    def share_part(d):
        peer = lax.rem(cell + d, n_cell)
        return remote(mine, others.at[d - 1], send_part.at[d], recv_part.at[d], cell=peer)

    def share_gram(d):
        peer = lax.rem(member + d, n_member)
        src = total.at[pl.ds(0, count)]
        return remote(src, gram.at[own], send_gram.at[d], recv_gram.at[d], member=peer)

    for d in range(1, n_member):
        share_pred(d).start()
    everyone[own, :] = pred[...]
    send_field(0)
    if fields > 1:
        stencil(1)
    for d in range(1, n_member):
        share_pred(d).wait()

    predicted = everyone[...]
    ybar = jnp.mean(predicted, axis=0, keepdims=True)
    live = lax.broadcasted_iota(jnp.int32, (1, slots), 1) < count_ref[0]
    weight = jnp.where(live, 1.0, 0.0) / jnp.sqrt(var_ref[...])
    scaled = (predicted - ybar) * weight
    local = (pred[...] - ybar) * weight
    innovation = jnp.broadcast_to(weight * (value_ref[...] - ybar), (8, slots))
    mine[...] = nt_dot(jnp.concatenate([local, innovation], axis=0), scaled)
    for d in range(1, n_cell):
        share_part(d).start()
    for f in range(2, fields):
        stencil(f)
    for d in range(1, n_cell):
        share_part(d).wait()
    summed = mine[...]
    for d in range(n_cell - 1):
        summed = summed + others[d]
    total[...] = summed
    for d in range(1, n_member):
        share_gram(d).start()
    for f in range(1, fields):
        send_field(f)
    gram[own, :] = total[pl.ds(0, count), :]
    pieces[member] = forecast[...]
    for d in range(1, n_member):
        share_gram(d).wait()

    lines = lax.broadcasted_iota(jnp.int32, (members, members), 0)
    columns = lax.broadcasted_iota(jnp.int32, (members, members), 1)
    identity = jnp.where(lines == columns, 1.0, 0.0).astype(jnp.float32)
    precision = gram[...] + (members - 1.0) * identity
    scale = jnp.sum(jnp.sum(precision * identity, axis=1, keepdims=True), axis=0, keepdims=True)
    upper[...] = precision / scale
    lower[...] = identity

    def newton(step, carry):
        y, z = split3(upper[...]), split3(lower[...])
        middle = split3(1.5 * identity - 0.5 * six_products(z, y))
        upper[...] = six_products(y, middle)
        lower[...] = six_products(middle, z)
        return carry

    for f in range(fields):
        lax.fori_loop(ROOT_STEPS * f // fields, ROOT_STEPS * (f + 1) // fields, newton, 0)
        forward_field(f)

    gain = total[pl.ds(count, 8), :]
    half_way = nt_dot(gain, lower[...])
    mean_weights = nt_dot(half_way, lower[...])[0:1, :] / scale
    root = jnp.sqrt((members - 1.0) / scale) * lower[own, :]
    blend = mean_weights + root
    transform = blend - jnp.mean(blend, axis=1, keepdims=True) + 1.0 / members
    coeff[...] = transform.astype(jnp.bfloat16)

    for f in range(fields):
        for d in range(chips):
            to_mate(d, f).wait()
        for d in range(1, chips):
            to_far(d, f).wait_send()

        def blend_row(r, carry):
            block = pieces[:, f, r].reshape(members, width)
            out_ref[f, r] = jnp.dot(coeff[...], block, preferred_element_type=jnp.float32)
            return carry

        lax.fori_loop(0, rows, blend_row, 0)

    for f in range(fields):

        @pl.when(has_north)
        def _():
            upward(f).wait_send()

        @pl.when(has_south)
        def _():
            downward(f).wait_send()


def shards(prior_sample_set, wind_table, regimes, obs_index, obs_count, obs_value, obs_var):
    n_cell, n_member = lax.axis_size("cell"), lax.axis_size("member")
    count, fields, rows, width = prior_sample_set.shape
    slots = obs_index.shape[1]
    members = count * n_member
    cells = prior_sample_set.transpose(1, 2, 0, 3)
    smem = pl.BlockSpec(memory_space=pltpu.SMEM)
    vmem = pl.BlockSpec(memory_space=pltpu.VMEM)
    single, half = jnp.float32, jnp.bfloat16
    edge = pltpu.VMEM((fields, HALO, count, width), half)
    square = pltpu.VMEM((members, members), single)
    part = (count + 8, members)
    dma = pltpu.SemaphoreType.DMA
    blended = pl.pallas_call(
        functools.partial(cycle_kernel, n_cell, n_member),
        in_specs=[smem] * 3 + [vmem] * 4,
        out_specs=vmem,
        out_shape=jax.ShapeDtypeStruct(cells.shape, single),
        scratch_shapes=[
            pltpu.SMEM((SUBSTEPS * 5, rows + 2 * HALO), single),
            pltpu.VMEM((rows, count, width), single),
            edge,
            edge,
            edge,
            edge,
            pltpu.VMEM((fields, rows, count, width), half),
            pltpu.VMEM((n_member, fields, rows, count, width), half),
            pltpu.VMEM((count, slots), single),
            pltpu.VMEM((count, members), half),
            pltpu.VMEM((members, slots), single),
            pltpu.VMEM(part, single),
            pltpu.VMEM((n_cell - 1,) + part, single),
            pltpu.VMEM(part, single),
            square,
            square,
            square,
        ]
        + [dma((fields,))] * 4
        + [dma((n_member,))] * 2
        + [dma((n_cell,))] * 2
        + [dma((n_member,))] * 2
        + [dma((n_member // 2, fields))] * 4,
        compiler_params=pltpu.CompilerParams(
            collective_id=0, has_side_effects=True, vmem_limit_bytes=VMEM_LIMIT
        ),
    )(regimes, wind_table, obs_count, obs_index, obs_value, obs_var, cells)
    return blended.transpose(2, 0, 1, 3)


def solution(mesh):
    return jax.shard_map(
        shards,
        mesh=mesh,
        in_specs=(
            P(("groups", "member"), None, "cell", None),
            P(),
            P("groups", None),
            P(("groups", "cell"), None),
            P(("groups", "cell")),
            P(("groups", "cell"), None),
            P(("groups", "cell"), None),
        ),
        out_specs=P(("groups", "member"), None, "cell", None),
        check_vma=False,
    )
```

time: 188 us -> 84.8 us (0.45)
  Pallas kernels: 0 us -> 70.5 us
  waiting for transfers between devices: 58.2 us -> 0 us
  matrix products: 43.5 us -> 0 us
  starting transfers between devices: 19.6 us -> 0 us
  other arithmetic: 19.1 us -> 0 us
  blocking collectives: 16 us -> 0 us
  between operations: 16.5 us -> 0.66 us
    pallas_call x0 -> x1, Pallas kernels: none -> 70.5 us  [shards(): pl.pallas_call(functools.partial(cycle_kernel, n_cell, n_member), in_spec...]
    dot_general x82 -> x0, matrix products: 43.5 us -> none  [the longest x24 14.3 us: newton_step(): jnp.dot(upper, middle, precision=lax.Precision.HIGHEST, preferred_element...]
    ppermute x8 -> x0, waiting for transfers between devices: 35.5 us -> none  [the longest x4 18.1 us: padded_2(): lax.ppermute(tail, axis, [(i, (i + 1) % count) for i in range(ends)])]
    psum x1 -> x0, waiting for transfers between devices: 22.7 us -> none  [shards(): gram, gain = lax.psum((gram_part, gain_part), 'cell')]
    ppermute x8 -> x0, starting transfers between devices: 19.6 us -> none  [the longest x4 14.4 us: padded_2(): lax.ppermute(tail, axis, [(i, (i + 1) % count) for i in range(ends)])]
    add x3 -> x0, other arithmetic: 10.5 us -> none  [stencil(): return result + diffusion * (north + south + east + west - 4.0 * centre)]
    psum x1 -> x0, blocking collectives: 8.64 us -> none  [shards(): gram, gain = lax.psum((gram_part, gain_part), 'cell')]
    all_gather x1 -> x0, blocking collectives: 7.35 us -> none  [shards(): predicted = lax.all_gather(local_pred, 'member', axis=0, tiled=True)]
  transfers between devices with their start and end apart: 10 -> 0, of which waited for: 9 -> 0; matrix products, arithmetic and copies ran while one was open for 23% -> 0% of each run, Pallas kernels for 0% -> 0%
where the time goes in v3:
time: 84.8 us; the launch traced here: 84.6 us
  Pallas kernels  70.5 us (83%)
  local copies, waits for them, and re-layouts  13.4 us (16%)
    pallas_call x1, Pallas kernels, shards(): pl.pallas_call(functools.partial(cycle_kernel, n_cell, n_member), in_spec...  70.5 us
    unnamed x3, local copies, waits for them, and re-layouts  8.06 us
    transpose x1, local copies, waits for them, and re-layouts, shards(): return blended.transpose(2, 0, 1, 3)  5.38 us

profile of v3, /device:TPU:0, one launch (start us, length us, event | category | flops | bytes accessed | tf_op | source)
XLA Modules:
  0.0 84.6 jit_solution(16085543973199145909)
XLA Ops:
  0.7 1.3 %copy.10.wind_ref = f32[8,2]{1,0:T(8,128)} copy(f32[8,2]{0,1:T(2,128)} %param.8) | data formatting | bytes 128 | tf_op args[1]
  2.0 1.3 %copy.9.regime_ref = s32[8,4]{1,0:T(8,128)} copy(s32[8,4]{0,1:T(4,128)} %param.9) | data formatting | bytes 256 | tf_op args[2]
  3.3 5.4 %copy.13 = f32[64,3,8,512]{3,0,2,1:T(8,128)} copy(f32[64,3,8,512]{3,2,1,0:T(8,128)} %param.7) | data formatting | bytes 6291456 | tf_op args[0]
  8.7 70.5 %shard_map.73 = f32[3,8,64,512]{3,2,1,0:T(8,128)} custom-call(s32[8,4]{1,0:T(8,128)} %copy.9.regime_ref, f32[8,2]{1,0:T(8,128)} %copy.10.wind_ref, s32[1]{0:T(128)S(6)} %copy.14.count_ref, s32[1,512]{1,0:T(1,128)} %index_ref.1, f32[1,512]{1,0:T(1,128)} %value_ref.1, f32[1,512]{1,0:T(1,128)} %var_ref.1, f32[3,8,64,512]{3,2,1,0:T(8,128)} %bitcast.5), custom_call_target="tpu_custom_call" | custom-call | tf_op jit(solution)/shard_map/pallas_call | solution.py:370
  79.2 5.4 %copy.11 = f32[64,3,8,512]{3,2,1,0:T(8,128)} copy(f32[64,3,8,512]{3,0,2,1:T(8,128)} %bitcast.4) | data formatting | bytes 6291456 | tf_op jit(solution)/shard_map/transpose | solution.py:403

commit v4 on v3

--- a/solution.py
+++ b/solution.py
@@ -14,7 +14,7 @@
 DIFFUSION = 0.02
 MESH = pl.DeviceIdType.MESH
 HIGHEST = lax.Precision.HIGHEST
-VMEM_LIMIT = 56 * 1024 * 1024
+VMEM_LIMIT = 26 * 1024 * 1024
 CHUNK = 16
 
 
@@ -58,7 +58,6 @@
     edge_down,
     south,
     north,
-    forecast,
     pieces,
     pred,
     coeff,
@@ -124,7 +123,7 @@
 
     def to_far(d, f):
         return remote(
-            forecast.at[f],
+            pieces.at[member, f],
             pieces.at[member, f],
             send_far.at[d, f],
             recv_far.at[d, f],
@@ -134,7 +133,7 @@
     def to_mate(d, f):
         owner = lax.rem(member + n_member - 2 * d, n_member)
         return remote(
-            forecast.at[f] if d == 0 else pieces.at[owner, f],
+            pieces.at[owner, f],
             pieces.at[owner, f],
             send_mate.at[d, f],
             recv_mate.at[d, f],
@@ -187,8 +186,8 @@
         inside = jnp.where((row >= 0) & (row < row_total), 1.0, 0.0)
         band = jnp.minimum(jnp.maximum(row, 0), row_total - 1) // BAND
         for s in range(SUBSTEPS):
-            regime = regime_ref[band, s]
-            cx, cy = wind_ref[regime, 0], wind_ref[regime, 1]
+            regime = regime_ref[s, band]
+            cx, cy = wind_ref[0, regime], wind_ref[1, regime]
             x_up, x_down = jnp.maximum(cx, 0.0), jnp.minimum(cx, 0.0)
             y_up, y_down = jnp.maximum(cy, 0.0), jnp.minimum(cy, 0.0)
             table[s * 5, i] = inside * (1.0 - 4.0 * DIFFUSION - x_up + x_down - y_up + y_down)
@@ -231,7 +230,7 @@
                     )
                 cells = fresh
             for i in range(rows):
-                forecast[f, i, at, :] = cells[HALO + i].astype(jnp.bfloat16)
+                pieces[member, f, i, at, :] = cells[HALO + i].astype(jnp.bfloat16)
                 if f == 0:
                     keep[i, at, :] = cells[HALO + i]
             return carry
@@ -299,7 +298,6 @@
     for f in range(1, fields):
         send_field(f)
     gram[own, :] = total[pl.ds(0, count), :]
-    pieces[member] = forecast[...]
     for d in range(1, n_member):
         share_gram(d).wait()
 
@@ -379,7 +377,6 @@
             edge,
             edge,
             edge,
-            pltpu.VMEM((fields, rows, count, width), half),
             pltpu.VMEM((n_member, fields, rows, count, width), half),
             pltpu.VMEM((count, slots), single),
             pltpu.VMEM((count, members), half),
@@ -399,7 +396,7 @@
         compiler_params=pltpu.CompilerParams(
             collective_id=0, has_side_effects=True, vmem_limit_bytes=VMEM_LIMIT
         ),
-    )(regimes, wind_table, obs_count, obs_index, obs_value, obs_var, cells)
+    )(regimes.T, wind_table.T, obs_count, obs_index, obs_value, obs_var, cells)
     return blended.transpose(2, 0, 1, 3)
 
 

time: 84.8 us -> 75.6 us (0.89)
  local copies, waits for them, and re-layouts: 13.4 us -> 7.25 us
  Pallas kernels: 70.5 us -> 67.5 us
    unnamed x3 -> x11, local copies, waits for them, and re-layouts: 8.06 us -> 3.76 us
    pallas_call x1, Pallas kernels: 70.5 us -> 67.5 us  [shards(): pl.pallas_call(functools.partial(cycle_kernel, n_cell, n_member), in_spec...]
    transpose x1, local copies, waits for them, and re-layouts: 5.38 us -> 3.49 us  [shards(): return blended.transpose(2, 0, 1, 3)]
where the time goes in v4:
time: 75.6 us; the launch traced here: 75.5 us
  Pallas kernels  67.5 us (89%)
  local copies, waits for them, and re-layouts  7.25 us (10%)
    pallas_call x1, Pallas kernels, shards(): pl.pallas_call(functools.partial(cycle_kernel, n_cell, n_member), in_spec...  67.5 us
    unnamed x11, local copies, waits for them, and re-layouts  3.76 us
    transpose x1, local copies, waits for them, and re-layouts, shards(): return blended.transpose(2, 0, 1, 3)  3.49 us

profile of v4, /device:TPU:0, one launch (start us, length us, event | category | flops | bytes accessed | tf_op | source)
XLA Modules:
  0.0 75.5 jit_solution(16782394843392616137)
XLA Ops:
  0.7 0.0 copy-start
  0.7 0.0 copy-start.1
  0.7 0.0 copy-start.2
  0.7 0.0 copy-start.3
  0.7 0.0 copy-start.4
  0.7 3.7 %copy.11 = f32[64,3,8,512]{3,0,2,1:T(8,128)S(1)} copy(f32[64,3,8,512]{3,2,1,0:T(8,128)} %param.7) | data formatting | bytes 6291456 | tf_op args[0]
  4.4 0.0 copy-done
  4.5 0.0 copy-done.1
  4.5 0.0 copy-done.2
  4.5 0.0 copy-done.3
  4.5 0.0 copy-done.4
  4.5 67.5 %shard_map.73 = f32[3,8,64,512]{3,2,1,0:T(8,128)S(1)} custom-call(s32[4,8]{1,0:T(4,128)S(1)} %bitcast.8, f32[2,8]{1,0:T(2,128)S(1)} %bitcast.9, s32[1]{0:T(128)S(6)} %copy.12.count_ref, s32[1,512]{1,0:T(1,128)S(1)} %copy-done.1, f32[1,512]{1,0:T(1,128)S(1)} %copy-done.2, f32[1,512]{1,0:T(1,128)S(1)} %copy-done.3, f32[3,8,64,512]{3,2,1,0:T(8,128)S(1)} %bitcast.7), custom_call_target="tpu_custom_call" | custom-call | tf_op jit(solution)/shard_map/pallas_call | solution.py:368
  72.0 3.5 %copy.9 = f32[64,3,8,512]{3,2,1,0:T(8,128)} copy(f32[64,3,8,512]{3,0,2,1:T(8,128)S(1)} %bitcast.6) | data formatting | bytes 6291456 | tf_op jit(solution)/shard_map/transpose | solution.py:400
Async XLA Ops:
  0.7 3.8 %copy-start = (s32[8,4]{0,1:T(4,128)S(1)}, s32[8,4]{0,1:T(4,128)}, u32[]{:S(2)}) copy-start(s32[8,4]{0,1:T(4,128)} %param.9) | copy-start | bytes 388
  0.7 3.8 %copy-start.1 = (s32[1,512]{1,0:T(1,128)S(1)}, s32[1,512]{1,0:T(1,128)}, u32[]{:S(2)}) copy-start(s32[1,512]{1,0:T(1,128)} %index_ref.1) | copy-start | bytes 6148
  0.7 3.8 %copy-start.2 = (f32[1,512]{1,0:T(1,128)S(1)}, f32[1,512]{1,0:T(1,128)}, u32[]{:S(2)}) copy-start(f32[1,512]{1,0:T(1,128)} %value_ref.1) | copy-start | bytes 6148
  0.7 3.8 %copy-start.3 = (f32[1,512]{1,0:T(1,128)S(1)}, f32[1,512]{1,0:T(1,128)}, u32[]{:S(2)}) copy-start(f32[1,512]{1,0:T(1,128)} %var_ref.1) | copy-start | bytes 6148
  0.7 3.8 %copy-start.4 = (f32[8,2]{0,1:T(2,128)S(1)}, f32[8,2]{0,1:T(2,128)}, u32[]{:S(2)}) copy-start(f32[8,2]{0,1:T(2,128)} %param.8) | copy-start | bytes 196

commit v5 on v4

--- a/solution.py
+++ b/solution.py
@@ -14,7 +14,7 @@
 DIFFUSION = 0.02
 MESH = pl.DeviceIdType.MESH
 HIGHEST = lax.Precision.HIGHEST
-VMEM_LIMIT = 26 * 1024 * 1024
+VMEM_LIMIT = 30 * 1024 * 1024
 CHUNK = 16
 
 
@@ -53,6 +53,7 @@
     x_ref,
     out_ref,
     table,
+    hits,
     keep,
     edge_up,
     edge_down,
@@ -237,15 +238,21 @@
 
         lax.fori_loop(0, count // CHUNK, one_chunk, 0)
 
+    column = lax.broadcasted_iota(jnp.int32, (width, slots), 0)
+
+    def mark_row(i, carry):
+        hit = jnp.where(column == index_ref[...] - i * width, 1.0, 0.0)
+        hits[i] = hit.astype(jnp.bfloat16)
+        return carry
+
+    lax.fori_loop(0, rows, mark_row, 0)
     stencil(0)
-    column = lax.broadcasted_iota(jnp.int32, (width, slots), 0)
     pred[...] = jnp.zeros_like(pred)
 
     def pick_row(i, carry):
-        hits = jnp.where(column == index_ref[...] - i * width, 1.0, 0.0)
         picked = jnp.dot(
             jnp.concatenate(split3(keep[i]), axis=0),
-            hits.astype(jnp.bfloat16),
+            hits[i],
             preferred_element_type=jnp.float32,
         )
         pred[...] += picked[:count] + picked[count : 2 * count] + picked[2 * count :]
@@ -372,6 +379,7 @@
         out_shape=jax.ShapeDtypeStruct(cells.shape, single),
         scratch_shapes=[
             pltpu.SMEM((SUBSTEPS * 5, rows + 2 * HALO), single),
+            pltpu.VMEM((rows, width, slots), half),
             pltpu.VMEM((rows, count, width), single),
             edge,
             edge,

time: 75.6 us -> 75.5 us (level)
  no operation moved by 1% of the time
where the time goes in v5:
time: 75.5 us; the launch traced here: 75.4 us
  Pallas kernels  67.4 us (89%)
  local copies, waits for them, and re-layouts  7.25 us (10%)
    pallas_call x1, Pallas kernels, shards(): pl.pallas_call(functools.partial(cycle_kernel, n_cell, n_member), in_spec...  67.4 us
    unnamed x11, local copies, waits for them, and re-layouts  3.76 us
    transpose x1, local copies, waits for them, and re-layouts, shards(): return blended.transpose(2, 0, 1, 3)  3.49 us

profile of v5, /device:TPU:0, one launch (start us, length us, event | category | flops | bytes accessed | tf_op | source)
XLA Modules:
  0.0 75.4 jit_solution(7847918787555060435)
XLA Ops:
  0.7 0.0 copy-start
  0.7 0.0 copy-start.1
  0.7 0.0 copy-start.2
  0.7 0.0 copy-start.3
  0.7 0.0 copy-start.4
  0.7 3.7 %copy.11 = f32[64,3,8,512]{3,0,2,1:T(8,128)S(1)} copy(f32[64,3,8,512]{3,2,1,0:T(8,128)} %param.7) | data formatting | bytes 6291456 | tf_op args[0]
  4.4 0.0 copy-done
  4.5 0.0 copy-done.1
  4.5 0.0 copy-done.2
  4.5 0.0 copy-done.3
  4.5 0.0 copy-done.4
  4.5 67.4 %shard_map.73 = f32[3,8,64,512]{3,2,1,0:T(8,128)S(1)} custom-call(s32[4,8]{1,0:T(4,128)S(1)} %bitcast.8, f32[2,8]{1,0:T(2,128)S(1)} %bitcast.9, s32[1]{0:T(128)S(6)} %copy.12.count_ref, s32[1,512]{1,0:T(1,128)S(1)} %copy-done.1, f32[1,512]{1,0:T(1,128)S(1)} %copy-done.2, f32[1,512]{1,0:T(1,128)S(1)} %copy-done.3, f32[3,8,64,512]{3,2,1,0:T(8,128)S(1)} %bitcast.7), custom_call_target="tpu_custom_call" | custom-call | tf_op jit(solution)/shard_map/pallas_call | solution.py:375
  71.9 3.5 %copy.9 = f32[64,3,8,512]{3,2,1,0:T(8,128)} copy(f32[64,3,8,512]{3,0,2,1:T(8,128)S(1)} %bitcast.6) | data formatting | bytes 6291456 | tf_op jit(solution)/shard_map/transpose | solution.py:408
Async XLA Ops:
  0.7 3.8 %copy-start = (s32[8,4]{0,1:T(4,128)S(1)}, s32[8,4]{0,1:T(4,128)}, u32[]{:S(2)}) copy-start(s32[8,4]{0,1:T(4,128)} %param.9) | copy-start | bytes 388
  0.7 3.8 %copy-start.1 = (s32[1,512]{1,0:T(1,128)S(1)}, s32[1,512]{1,0:T(1,128)}, u32[]{:S(2)}) copy-start(s32[1,512]{1,0:T(1,128)} %index_ref.1) | copy-start | bytes 6148
  0.7 3.8 %copy-start.2 = (f32[1,512]{1,0:T(1,128)S(1)}, f32[1,512]{1,0:T(1,128)}, u32[]{:S(2)}) copy-start(f32[1,512]{1,0:T(1,128)} %value_ref.1) | copy-start | bytes 6148
  0.7 3.8 %copy-start.3 = (f32[1,512]{1,0:T(1,128)S(1)}, f32[1,512]{1,0:T(1,128)}, u32[]{:S(2)}) copy-start(f32[1,512]{1,0:T(1,128)} %var_ref.1) | copy-start | bytes 6148
  0.7 3.8 %copy-start.4 = (f32[8,2]{0,1:T(2,128)S(1)}, f32[8,2]{0,1:T(2,128)}, u32[]{:S(2)}) copy-start(f32[8,2]{0,1:T(2,128)} %param.8) | copy-start | bytes 196
